TPU v7x, 128 devices: a whole 4x4x4 slice. The times are simulated.
128 devices in a mesh: gx: 8 (over z_hi, x), gy: 16 (over z_lo, y, core).
Axes of the slice: x: 4, y: 4, z: 4 (z_hi: 2, z_lo: 2; z = z_hi * 2 + z_lo), core: 2. Of those that a mesh axis runs over, the one named last changes fastest.
Arguments:
- coarse: bfloat16 [12, 128, 512], P(None, ('gx', 'gy')), may hold values from -6 to 6
- weight_one: bfloat16 [3, 3, 12, 64], replicated, may hold values from -0.625 to 0.625
- weight_two: bfloat16 [3, 3, 64, 64], replicated, may hold values from -0.25 to 0.25
- weight_three: bfloat16 [3, 3, 64, 256], replicated, may hold values from -0.25 to 0.25
- weight_four: bfloat16 [3, 3, 64, 256], replicated, may hold values from -0.25 to 0.25
- weight_five: bfloat16 [3, 3, 64, 12], replicated, may hold values from -0.25 to 0.25
- bias_one: float32 [64], replicated, may hold values from -3 to 3
- bias_two: float32 [64], replicated, may hold values from -3 to 3
- bias_three: float32 [256], replicated, may hold values from -3 to 3
- bias_four: float32 [256], replicated, may hold values from -3 to 3
- bias_five: float32 [12], replicated, may hold values from -3 to 3
- cotangent: bfloat16 [12, 512, 2048], P(None, 'gx', 'gy'), may hold values from -6 to 6
Outputs:
- fine: float32 [12, 512, 2048], P(None, 'gx', 'gy')
- grad_w1: float32 [3, 3, 12, 64], replicated
- grad_w2: float32 [3, 3, 64, 64], replicated
- grad_w3: float32 [3, 3, 64, 256], replicated
- grad_w4: float32 [3, 3, 64, 256], replicated
- grad_w5: float32 [3, 3, 64, 12], replicated
- grad_b1: float32 [64], replicated
- grad_b2: float32 [64], replicated
- grad_b3: float32 [256], replicated
- grad_b4: float32 [256], replicated
- grad_b5: float32 [12], replicated
All inputs are finite; a program needn't handle non-finite values.
Results may differ from a plain program's by a relative error of at most 0.013.
Values may be sent and summed in bfloat16 or wider, within the bound.
A program may use at most 128 MiB of HBM per device.

v0:
```python
import functools

import jax
import jax.numpy as jnp
from jax import lax
from jax.experimental import pallas as pl
from jax.experimental.pallas import tpu as pltpu
from jax.sharding import PartitionSpec as P

MESH_ID = pl.DeviceIdType.MESH
PACK = 3072
HALF = PACK // 2
THIRD = HALF // 3
PARTS = (THIRD // 4, THIRD // 16, THIRD // 64)


def coordinates():
    gx = lax.axis_index("gx")
    gy = lax.axis_index("gy")
    return (gx % 4, (gy // 2) % 4, (gx // 4) * 2 + gy // 8), gy % 2


def device_at(place, core):
    x, y, z = place
    return ((z // 2) * 4 + x, (z % 2) * 8 + y * 2 + core)


def along(place, axis, step):
    moved = list(place)
    moved[axis] = (place[axis] + step) % 4
    return moved


def rows_at(start, count):
    return pl.ds(pl.multiple_of(start, 8), count)


def total_kernel(
    scale,
    pack,
    out_w1,
    out_w2,
    out_w3,
    out_w4,
    out_w5,
    out_b1,
    out_b2,
    out_b3,
    out_b4,
    out_b5,
    pair_in,
    pair_sum,
    in_a,
    sum_a,
    in_b,
    sum_b,
    in_c,
    whole,
    pair_send,
    pair_recv,
    down_send,
    down_recv,
    up_send,
    up_recv,
):
    place, core = coordinates()
    partner = device_at(place, 1 - core)
    barrier = pltpu.get_barrier_semaphore()
    peers = [partner] + [
        device_at(along(place, axis, step), core) for axis in range(3) for step in (1, 2, 3)
    ]
    for peer in peers:
        pl.semaphore_signal(barrier, inc=1, device_id=peer, device_id_type=MESH_ID)
    pl.semaphore_wait(barrier, len(peers))

    def send(src, dst, send_sem, recv_sem, peer):
        copy = pltpu.make_async_remote_copy(
            src_ref=src,
            dst_ref=dst,
            send_sem=send_sem,
            recv_sem=recv_sem,
            device_id=peer,
            device_id_type=MESH_ID,
        )
        copy.start()
        return copy

    sent = []
    pairs = []
    for third in range(3):
        pairs.append(
            send(
                pack.at[rows_at((1 - core) * HALF + third * THIRD, THIRD)],
                pair_in.at[pl.ds(third * THIRD, THIRD)],
                pair_send.at[third],
                pair_recv.at[third],
                partner,
            )
        )
    stage_in = (in_a, in_b, in_c)
    stage_from = (pair_sum, sum_a, sum_b)
    spans = (THIRD, PARTS[0], PARTS[1])

    def scatter(third, stage):
        axis = (third + stage) % 3
        part = PARTS[stage]
        copies = []
        for step in (1, 2, 3):
            quarter = (place[axis] + step) % 4
            copies.append(
                send(
                    stage_from[stage].at[rows_at(third * spans[stage] + quarter * part, part)],
                    stage_in[stage].at[third, step - 1],
                    down_send.at[stage, third, step - 1],
                    down_recv.at[stage, third, step - 1],
                    device_at(along(place, axis, step), core),
                )
            )
        return copies

    def collect(third, stage, copies):
        axis = (third + stage) % 3
        part = PARTS[stage]
        value = stage_from[stage][rows_at(third * spans[stage] + place[axis] * part, part), :]
        for step in (1, 2, 3):
            copies[step - 1].wait_recv()
            value = value + stage_in[stage][third, step - 1]
        return value

    def row_of(third, level):
        row = core * HALF + third * THIRD
        for stage in range(level):
            row = row + place[(third + stage) % 3] * PARTS[stage]
        return row

    flying = []
    for third in range(3):
        pairs[third].wait_recv()
        own = pack[rows_at(core * HALF + third * THIRD, THIRD), :]
        pair_sum[pl.ds(third * THIRD, THIRD), :] = own + pair_in[pl.ds(third * THIRD, THIRD), :]
        flying.append(scatter(third, 0))
    for stage in range(2):
        arrived = flying
        sent = sent + flying
        flying = []
        for third in range(3):
            part = PARTS[stage]
            stage_from[stage + 1][pl.ds(third * part, part), :] = collect(
                third, stage, arrived[third]
            )
            flying.append(scatter(third, stage + 1))
    sent = sent + flying

    def gather(third, stage):
        axis = (third + stage) % 3
        part = PARTS[stage]
        block = whole.at[rows_at(row_of(third, stage + 1), part)]
        return [
            send(
                block,
                block,
                up_send.at[stage, third, step - 1],
                up_recv.at[stage, third, step - 1],
                device_at(along(place, axis, step), core),
            )
            for step in (1, 2, 3)
        ]

    rising = []
    for third in range(3):
        whole[rows_at(row_of(third, 3), PARTS[2]), :] = collect(third, 2, flying[third])
        rising.append(gather(third, 2))
    for stage in (1, 0):
        arrived = rising
        sent = sent + rising
        rising = []
        for third in range(3):
            for copy in arrived[third]:
                copy.wait_recv()
            rising.append(gather(third, stage))
    sent = sent + rising
    finals = []
    for third in range(3):
        for copy in rising[third]:
            copy.wait_recv()
        block = whole.at[rows_at(row_of(third, 0), THIRD)]
        finals.append(
            send(block, block, pair_send.at[3 + third], pair_recv.at[3 + third], partner)
        )
    for copy in finals:
        copy.wait_recv()
    for copies in sent:
        for copy in copies:
            copy.wait_send()
    for copy in pairs + finals:
        copy.wait_send()

    for index, target in ((0, out_w4), (1152, out_w3)):
        target[:, 0:128] = whole[index : index + 576, :] * scale
        target[:, 128:256] = whole[index + 576 : index + 1152, :] * scale
    out_w2[...] = whole[2304:2880, 0:64] * scale
    out_w5[...] = whole[2304:2880, 64:76] * scale
    for tap in range(9):
        out_w1[tap] = whole[2880 + 12 * tap : 2892 + 12 * tap, 0:64] * scale
    for index, target in ((2992, out_b4), (2994, out_b3)):
        target[:, 0:128] = whole[index : index + 1, :] * scale
        target[:, 128:256] = whole[index + 1 : index + 2, :] * scale
    out_b2[...] = whole[2996:2997, 0:64] * scale
    out_b1[...] = whole[2996:2997, 64:128] * scale
    out_b5[...] = whole[2997:2998, 0:12] * scale


def totals_of(pack, scale):
    shapes = ((9, 12, 64), (576, 64), (576, 256), (576, 256), (576, 12))
    shapes = shapes + ((1, 64), (1, 64), (1, 256), (1, 256), (1, 12))
    vmem = pl.BlockSpec(memory_space=pltpu.VMEM)
    scratch = [pltpu.VMEM((HALF, 128), jnp.float32) for _ in range(2)]
    for part in PARTS[:2]:
        scratch.append(pltpu.VMEM((3, 3, part, 128), jnp.float32))
        scratch.append(pltpu.VMEM((3 * part, 128), jnp.float32))
    scratch.append(pltpu.VMEM((3, 3, PARTS[2], 128), jnp.float32))
    scratch.append(pltpu.VMEM((PACK, 128), jnp.float32))
    scratch += [pltpu.SemaphoreType.DMA((6,))] * 2 + [pltpu.SemaphoreType.DMA((3, 3, 3))] * 4
    return pl.pallas_call(
        functools.partial(total_kernel, scale),
        out_shape=[jax.ShapeDtypeStruct(shape, jnp.float32) for shape in shapes],
        in_specs=[vmem],
        out_specs=[vmem] * 10,
        scratch_shapes=scratch,
        compiler_params=pltpu.CompilerParams(collective_id=1, has_side_effects=True),
        name="grad_totals",
    )(pack)


def gather_kernel(coarse, cot, rows_out, cot_out, keep_sem, row_send, row_recv, far_send, far_recv, cot_send, cot_recv):
    gx = lax.axis_index("gx")
    gy = lax.axis_index("gy")

    def peer(step_x, step_y):
        return ((gx + step_x + 8) % 8, (gy + step_y + 16) % 16)

    barrier = pltpu.get_barrier_semaphore()
    for step_x in (-1, 0, 1):
        for step_y in range(16):
            if step_x != 0 or step_y != 0:
                pl.semaphore_signal(
                    barrier, inc=1, device_id=peer(step_x, step_y), device_id_type=MESH_ID
                )
    locals_ = [
        pltpu.make_async_copy(
            cot, cot_out.at[:, pl.ds(16, 64), pl.ds(128, 128)], keep_sem.at[0]
        ),
        pltpu.make_async_copy(
            coarse.at[:, pl.ds(window(gy), 256)], rows_out.at[6 + gy], keep_sem.at[1]
        ),
    ]
    for copy in locals_:
        copy.start()
    pl.semaphore_wait(barrier, 47)

    def remote(src, dst, send_sem, recv_sem, target):
        return pltpu.make_async_remote_copy(
            src_ref=src,
            dst_ref=dst,
            send_sem=send_sem,
            recv_sem=recv_sem,
            device_id=target,
            device_id_type=MESH_ID,
        )

    def row_copy(step, dst_row, send_sem, recv_sem, step_x):
        target = peer(step_x, step)
        return remote(
            coarse.at[:, pl.ds(window(target[1]), 256)],
            rows_out.at[dst_row],
            send_sem,
            recv_sem,
            target,
        )

    copies = []
    parts = ((16, 48, 0), (64, 0, 16), (16, 0, 80))
    for index_x, step_x in enumerate((1, 0, -1)):
        count, src_row, dst_row = parts[index_x]
        for index_y, step_y in enumerate((1, 0, -1)):
            if step_x == 0 and step_y == 0:
                continue
            copies.append(
                remote(
                    cot.at[:, pl.ds(src_row, count), :],
                    cot_out.at[:, pl.ds(dst_row, count), pl.ds(128 * index_y, 128)],
                    cot_send.at[index_x, index_y],
                    cot_recv.at[index_x, index_y],
                    peer(step_x, step_y),
                )
            )
    for step in range(1, 16):
        copies.append(row_copy(step, 6 + gy, row_send.at[step], row_recv.at[step], 0))
    for copy in copies:
        copy.start()

    def far(step_x, dst_row, slot):
        return [
            row_copy(step, dst_row, far_send.at[step], far_recv.at[slot], step_x)
            for step in range(16)
        ]

    @pl.when(gy < 6)
    def _():
        for copy in far(-1, 22 + gy, 6 + gy):
            copy.start()

    @pl.when(gy >= 10)
    def _():
        for copy in far(1, gy - 10, gy - 10):
            copy.start()

    for copy in locals_:
        copy.wait()
    for copy in copies[:8]:
        copy.wait()
    for step in range(1, 16):
        row_copy(step, 6 + (gy - step + 16) % 16, row_send.at[step], row_recv.at[step], 0).wait()
    for slot in range(12):
        dst_row = slot if slot < 6 else 16 + slot
        row_copy(1, dst_row, far_send.at[0], far_recv.at[slot], 0).wait_recv()

    @pl.when(gy < 6)
    def _():
        for copy in far(-1, 22 + gy, 6 + gy):
            copy.wait_send()

    @pl.when(gy >= 10)
    def _():
        for copy in far(1, gy - 10, gy - 10):
            copy.wait_send()


def window(gy):
    return pl.multiple_of(jnp.clip(jnp.right_shift(gy * 32 - 8, 7), 0, 2) * 128, 128)


def gather_of(coarse, cot):
    vmem = pl.BlockSpec(memory_space=pltpu.VMEM)
    dma = pltpu.SemaphoreType.DMA
    return pl.pallas_call(
        gather_kernel,
        out_shape=[
            jax.ShapeDtypeStruct((28, 16, 256), jnp.bfloat16),
            jax.ShapeDtypeStruct((12, 96, 384), jnp.bfloat16),
        ],
        in_specs=[vmem] * 2,
        out_specs=[vmem] * 2,
        scratch_shapes=[dma((2,)), dma((16,)), dma((16,)), dma((16,)), dma((12,)), dma((3, 3)), dma((3, 3))],
        compiler_params=pltpu.CompilerParams(collective_id=0, has_side_effects=True),
        name="rim_gather",
    )(coarse, cot)


STRIDE = 48
ROWS = 30
SPAN = ROWS * STRIDE
BF = jnp.bfloat16
F32 = jnp.float32


def start_of(halo):
    return (7 - halo) * STRIDE - 16


def count_of(halo):
    return (16 + 2 * halo) * STRIDE + 32


def mm(lhs, rhs):
    return lax.dot_general(lhs, rhs, (((1,), (0,)), ((), ())), preferred_element_type=F32)


def mm_nt(lhs, rhs):
    return lax.dot_general(lhs, rhs, (((1,), (1,)), ((), ())), preferred_element_type=F32)


def mm_tn(lhs, rhs):
    return lax.dot_general(lhs, rhs, (((0,), (0,)), ((), ())), preferred_element_type=F32)


def iota(shape, dim):
    return lax.broadcasted_iota(jnp.int32, shape, dim)


def over(value, divisor):
    return lax.shift_right_logical(value * ((1 << 16) // divisor + 1), 16)


def one_hot(flag):
    return jnp.where(flag, 1.0, 0.0).astype(F32).astype(BF)


def three_parts(value):
    high = value.astype(BF)
    rest = value - high.astype(F32)
    middle = rest.astype(BF)
    return high, middle, (rest - middle.astype(F32)).astype(BF)


def exact_right(value, selector):
    parts = three_parts(value)
    return (mm(parts[2], selector) + mm(parts[1], selector)) + mm(parts[0], selector)


def blocks(total, chunk, body):
    def step(index, carry):
        body(pl.multiple_of(index * chunk, 16))
        return carry

    lax.fori_loop(0, total // chunk, step, 0)


def slab(start, count):
    if isinstance(start, int):
        return pl.ds(start, count)
    return pl.ds(pl.multiple_of(start, 16), count)


def inner(ref, shift, lanes):
    first = 7 + shift
    picked = [ref[(first + row) * STRIDE : (first + row) * STRIDE + 32, lanes] for row in range(16)]
    return jnp.concatenate(picked, axis=0)


ROW_SOURCE = (((1, -1), (0, 0), (1, 0)), ((0, 0), (1, 0), (0, 1)))
BACK_SOURCE = ((1, -1), (0, 0), (1, 0), (0, 1))
FINE_SOURCE = ((3, -1), (0, 0), (1, 0), (2, 0), (3, 0), (0, 1))
PAIR_ORDER = (1, 2, 3, 0)
FINE_ORDER = (1, 2, 3, 4, 5, 0)


def compute_kernel(
    where_am_i,
    rows_in,
    cot_in,
    w1,
    w2,
    w3,
    w4,
    w5,
    b1,
    b2,
    b3,
    b4,
    b5,
    fine,
    pack,
    mask,
    t_c1,
    m_c1,
    x1,
    t64,
    x2,
    x3,
    t3,
    x4,
    t4,
    x5,
    ay,
    t_cot,
    m_cot,
    xc,
    g5,
    t_g4,
    g4,
    t_g3,
    g3,
    g2,
    v1,
    v3,
    v4,
    v4f,
    v4b,
    v3b,
    v2b,
    v5f,
    v5b,
    acc,
    z5,
    turned,
    lined,
    wide,
):
    gx, gy = where_am_i()
    base_row = gx * 16
    base_col = gy * 32

    place = iota((SPAN, 128), 0)
    line = over(place, STRIDE)
    col = place - line * STRIDE
    left = jnp.where(col >= 40, 1, 0)
    row = line - 7 + left + base_row
    col = col - left * STRIDE + base_col
    ok = (row >= 0) & (row < 128) & (col >= 0) & (col < 512)
    mask[...] = jnp.where(ok, 1.0, 0.0)

    def kept(start, count):
        return mask[slab(start, count), 0:1]

    lane = iota((256, 256), 1)
    natural = iota((256, 256), 0)
    wanted = (lane - over(lane, 64) * 64) * 4 + over(lane, 64)
    to_phase = one_hot(natural == wanted)
    wanted_back = (natural - over(natural, 64) * 64) * 4 + over(natural, 64)
    to_natural = one_hot(lane == wanted_back)
    v3[...] = mm(w3[...], to_phase).astype(BF)
    v4[...] = mm(w4[...], to_phase).astype(BF)
    bias3 = exact_right(jnp.broadcast_to(b3[...], (8, 256)), to_phase)[0:1]
    bias4 = exact_right(jnp.broadcast_to(b4[...], (8, 256)), to_phase)[0:1]

    v1[...] = jnp.zeros(v1.shape, BF)
    for r in range(3):
        for s in range(3):
            v1[s * 48 + r * 16 : s * 48 + r * 16 + 12, :] = w1[r * 3 + s]
    for r in range(3):
        for position, c4 in enumerate(PAIR_ORDER):
            for q in range(2):
                s = c4 - q
                target = (slice(position * 64, position * 64 + 64), slice(q * 256, q * 256 + 256))
                if 0 <= s <= 2:
                    v4f[r, target[0], target[1]] = v4[(r * 3 + s) * 64 : (r * 3 + s) * 64 + 64, :]
                else:
                    v4f[r, target[0], target[1]] = jnp.zeros((64, 256), BF)
    for u in range(4):
        for a in range(2):
            for b in range(2):
                for position, v in enumerate(PAIR_ORDER):
                    r, s = a + 2 - u, b + 2 - v
                    at = (slice((2 * a + b) * 64, (2 * a + b) * 64 + 64),)
                    at = at + (slice(position * 256, position * 256 + 256),)
                    if 0 <= r <= 2 and 0 <= s <= 2:
                        tap = (r * 3 + s) * 64
                        v4b[u, at[0], at[1]] = v4[tap : tap + 64, :]
                    else:
                        v4b[u, at[0], at[1]] = jnp.zeros((64, 256), BF)
    for u in range(3):
        for v in range(3):
            tap = ((2 - u) * 3 + 2 - v) * 64
            v3b[u, :, v * 256 : v * 256 + 256] = v3[tap : tap + 64, :]
            v2b[u, :, v * 64 : v * 64 + 64] = w2[tap : tap + 64, :]

    lanes5 = iota((16, 192), 1)
    spread = one_hot((lanes5 - over(lanes5, 12) * 12) == iota((16, 192), 0))[0:12]
    wide[:, 0:192] = mm(w5[...], spread)
    lanes5 = iota((64, 192), 1)
    cell5 = over(lanes5, 12)
    col5 = over(cell5, 4)
    row5 = cell5 - col5 * 4
    for t in range(6):
        for position, v in enumerate(FINE_ORDER):
            value = jnp.zeros((64, 192), F32)
            for r in range(max(0, t - 3), min(2, t) + 1):
                for s in range(max(0, v - 3), min(2, v) + 1):
                    tap = (r * 3 + s) * 64
                    value = jnp.where(
                        (row5 == t - r) & (col5 == v - s), wide[tap : tap + 64, 0:192], value
                    )
            v5f[t, position * 64 : position * 64 + 64, :] = value.astype(BF)
    lanes6 = iota((16, 432), 1)
    spread = one_hot((lanes6 - over(lanes6, 12) * 12) == iota((16, 432), 0))[0:12]
    wide[...] = mm(w5[...], spread)
    lanes6 = iota((64, 432), 1)
    cell6 = over(lanes6, 12)
    col6 = over(cell6, 6)
    row6 = cell6 - col6 * 6
    for big_r in range(4):
        for big_c in range(4):
            value = jnp.zeros((64, 432), F32)
            for r in range(3):
                for s in range(3):
                    tap = (r * 3 + s) * 64
                    value = jnp.where(
                        (row6 == big_r + 2 - r) & (col6 == big_c + 2 - s),
                        wide[tap : tap + 64, :],
                        value,
                    )
            at = (big_r * 4 + big_c) * 64
            v5b[at : at + 64, :] = value.astype(BF)

    spot = iota((144, 256), 0)
    tap_col = over(spot, 48)
    want = spot - tap_col * 48 - 8 + tap_col - 1 + base_col
    first = jnp.clip(jnp.right_shift(base_col - 8, 7), 0, 2) * 128
    pick = one_hot((want == iota((144, 256), 1) + first) & (want >= 0) & (want < 512))
    tall = iota((448, 256), 0)
    tall_row = over(tall, 16) - 6 + base_row
    known = rows_in[...].reshape(448, 256).astype(F32)
    known = jnp.where((tall_row >= 0) & (tall_row < 128), known, 0.0).astype(BF)
    m_c1[...] = mm_nt(pick, known)
    t_c1[...] = jnp.zeros(t_c1.shape, F32)
    for i in range(-5, 21):
        for s in range(3):
            at = (i + 7) * STRIDE - 8
            t_c1[at : at + 48, s * 48 : s * 48 + 48] = m_c1[
                s * 48 : s * 48 + 48, (i + 5) * 16 : (i + 5) * 16 + 48
            ]
    x1[...] = t_c1[...].astype(BF)

    for ref in (t64, t3, t_g3, t_g4):
        ref[0:8, :] = jnp.zeros((8, ref.shape[1]), F32)
    for ref in (t3, t_g3, t_g4):
        ref[ref.shape[0] - 8 :, :] = jnp.zeros((8, ref.shape[1]), F32)
    for big_r in range(4):
        t4[big_r, 0:8, :] = jnp.zeros((8, 256), F32)
        t4[big_r, 1096:1104, :] = jnp.zeros((8, 256), F32)
    begin, count = start_of(3), count_of(3)
    for a in range(2):
        x4[a, begin - 48 : begin, :] = jnp.zeros((48, 256), BF)
        x4[a, begin + count : begin + count + 48, :] = jnp.zeros((48, 256), BF)

    def three_shifts(target, begin, count):
        t64[8 + count : 16 + count, :] = jnp.zeros((8, 64), F32)
        for s in range(3):
            target[begin : begin + count, s * 64 : s * 64 + 64] = t64[7 + s : 7 + s + count, :].astype(BF)

    begin, count = start_of(5), count_of(5)

    def one(at):
        z = mm(x1[slab(begin + at, 256), :], v1[...]) + b1[...]
        t64[pl.ds(pl.multiple_of(8 + at, 8), 256), :] = (
            jnp.tanh(z) * kept(begin + at, 256)
        )

    blocks(count, 256, one)
    three_shifts(x2, begin, count)

    begin2, count2 = start_of(4), count_of(4)

    def two(at):
        z = b2[...]
        for r in range(3):
            z = z + mm(x2[slab(begin2 + 48 * (r - 1) + at, 592), :], w2[192 * r : 192 * r + 192, :])
        t64[pl.ds(pl.multiple_of(8 + at, 8), 592), :] = jnp.tanh(z) * kept(begin2 + at, 592)

    blocks(count2, 592, two)
    three_shifts(x3, begin2, count2)

    begin3, count3 = start_of(3), count_of(3)

    def three(at):
        z = bias3
        for r in range(3):
            z = z + mm(x3[slab(begin3 + 48 * (r - 1) + at, 272), :], v3[192 * r : 192 * r + 192, :])
        t3[pl.ds(pl.multiple_of(8 + at, 8), 272), :] = jnp.tanh(z) * kept(begin3 + at, 272)

    blocks(count3, 272, three)
    for a in range(2):
        at = slice(begin3, begin3 + count3)
        x4[a, at, 0:128] = t3[8 : 8 + count3, a * 128 : a * 128 + 128].astype(BF)
        x4[a, at, 128:192] = t3[9 : 9 + count3, a * 128 : a * 128 + 64].astype(BF)
        x4[a, at, 192:256] = t3[7 : 7 + count3, a * 128 + 64 : a * 128 + 128].astype(BF)

    def four(at):
        for p in range(2):
            z = jnp.concatenate([bias4, bias4], axis=1)
            for r in range(3):
                a, d = ROW_SOURCE[p][r]
                z = z + mm(x4[a, slab(begin3 + 48 * d + at, 272), :], v4f[r])
            z = jnp.tanh(z) * kept(begin3 + at, 272)
            for half in range(2):
                for q in range(2):
                    t4[2 * p + half, pl.ds(pl.multiple_of(8 + at, 8), 272), q * 128 : q * 128 + 128] = z[
                        :, q * 256 + half * 128 : q * 256 + half * 128 + 128
                    ]

    blocks(count3, 272, four)
    for big_r in range(4):
        at = slice(begin3, begin3 + count3)
        x5[big_r, at, 0:256] = t4[big_r, 8 : 8 + count3, :].astype(BF)
        x5[big_r, at, 256:320] = t4[big_r, 9 : 9 + count3, 0:64].astype(BF)
        x5[big_r, at, 320:384] = t4[big_r, 7 : 7 + count3, 192:256].astype(BF)

    z = jnp.zeros((512, 192), F32)
    for t in range(6):
        big_r, d = FINE_SOURCE[t]
        z = z + mm(inner(x5.at[big_r], d, slice(0, 384)), v5f[t])
    z5[...] = z
    for i in range(16):
        for big_c in range(4):
            turned[big_c * 32 : big_c * 32 + 32, i * 48 : i * 48 + 48] = z5[
                i * 32 : i * 32 + 32, big_c * 48 : big_c * 48 + 48
            ]
    spot = iota((128, 128), 0)
    column = over(spot, 32)
    weave = one_hot(iota((128, 128), 1) == (spot - column * 32) * 4 + column)
    parts = three_parts(turned[...])
    lined[...] = (mm_tn(parts[2], weave) + mm_tn(parts[1], weave)) + mm_tn(parts[0], weave)
    for o in range(12):
        fine[o] = lined[pl.ds(o, 64, stride=12), :] + b5[0:1, o : o + 1]

    fine_row = iota((96, 128), 0) - 16 + gx * 64
    row_ok = (fine_row >= 0) & (fine_row < 512)
    for o in range(12):
        for third in range(3):
            value = cot_in[o, :, third * 128 : third * 128 + 128].astype(F32)
            ay[third, pl.ds(o, 96, stride=12), :] = jnp.where(row_ok, value, 0.0)
    spot = iota((288, 384), 0)
    tap_col = over(spot, 48)
    want = (spot - tap_col * 48 - 8) * 4 + tap_col - 1
    real = want + gy * 128
    pick = one_hot((iota((288, 384), 1) == want + 128) & (real >= 0) & (real < 2048))
    value = None
    for third in range(3):
        term = mm_nt(pick[:, third * 128 : third * 128 + 128], ay[third].astype(BF))
        value = term if value is None else value + term
    m_cot[...] = value
    t_cot[...] = jnp.zeros(t_cot.shape, F32)
    for i in range(-3, 19):
        for v in range(6):
            at = (i + 7) * STRIDE - 8
            t_cot[at : at + 48, v * 72 : v * 72 + 72] = m_cot[
                v * 48 : v * 48 + 48, (4 * i + 15) * 12 : (4 * i + 15) * 12 + 72
            ]
    xc[...] = t_cot[...].astype(BF)
    for big_c in range(4):
        at = (big_c + 1) * 72 + 12
        g5[:, big_c * 48 : big_c * 48 + 48] = inner(t_cot, 0, slice(at, at + 48)).astype(BF)

    lanes5 = iota((384, 192), 1)
    cell5 = over(lanes5, 12)
    col5 = over(cell5, 4)
    row5 = cell5 - col5 * 4
    for r in range(3):
        acc[r, 0:384, 0:192] = jnp.zeros((384, 192), F32)
    for t in range(6):
        big_r, d = FINE_SOURCE[t]
        z5[0:384, :] = mm_tn(inner(x5.at[big_r], d, slice(0, 384)), g5[...])
        for r in range(max(0, t - 3), min(2, t) + 1):
            acc[r, 0:384, 0:192] = jnp.where(row5 == t - r, z5[0:384, :], acc[r, 0:384, 0:192])
    fold_lane = iota((192, 128), 0)
    fold = one_hot((fold_lane - over(fold_lane, 12) * 12) + 64 == iota((192, 128), 1))
    col5 = col5[0:64]
    for r in range(3):
        for s in range(3):
            value = jnp.zeros((64, 192), F32)
            for big_c in range(4):
                position = FINE_ORDER.index(big_c + s)
                value = jnp.where(
                    col5 == big_c, acc[r, position * 64 : position * 64 + 64, 0:192], value
                )
            at = 2304 + (r * 3 + s) * 64
            pack[at : at + 64, :] = exact_right(value, fold)
    sums5 = jnp.sum(g5[...].astype(F32), axis=0, keepdims=True)
    fold_zero = one_hot((fold_lane - over(fold_lane, 12) * 12) == iota((192, 128), 1))
    pack[2988:3072, :] = jnp.zeros((84, 128), F32)
    pack[2997:2998, :] = exact_right(jnp.broadcast_to(sums5, (8, 192)), fold_zero)[0:1]

    def back_four(at):
        here = slab(begin3 + at, 272)
        keep = kept(begin3 + at, 272)
        for big_r in range(4):
            value = mm_nt(xc[here, :], v5b[big_r * 256 : big_r * 256 + 256, :])
            act = x5[big_r, here, 0:256].astype(F32)
            t_g4[pl.ds(pl.multiple_of(8 + at, 8), 272), big_r * 256 : big_r * 256 + 256] = (
                value * (1.0 - act * act) * keep
            )

    blocks(count3, 272, back_four)
    for p in range(2):
        at = slice(begin3, begin3 + count3)
        for half in range(2):
            src = (2 * p + half) * 256
            dst = half * 128
            for q in range(2):
                g4[p, at, q * 256 + dst : q * 256 + dst + 128] = t_g4[
                    8 : 8 + count3, src + q * 128 : src + q * 128 + 128
                ].astype(BF)
            g4[p, at, 512 + dst : 640 + dst] = t_g4[9 : 9 + count3, src : src + 128].astype(BF)
            g4[p, at, 768 + dst : 896 + dst] = t_g4[7 : 7 + count3, src + 128 : src + 256].astype(BF)

    sums4 = jnp.zeros((1, 256), F32)
    for p in range(2):
        value = inner(g4.at[p], 0, slice(0, 512))
        sums = jnp.sum(value.astype(F32), axis=0, keepdims=True)
        sums4 = sums4 + sums[:, 0:256] + sums[:, 256:512]
        for r in range(3):
            a, d = ROW_SOURCE[p][r]
            term = mm_tn(inner(x4.at[a], d, slice(0, 256)), value)
            if p == 0:
                acc[r, 0:256, :] = term
            else:
                acc[r, 0:256, :] = acc[r, 0:256, :] + term
    for r in range(3):
        for s in range(3):
            one_at = PAIR_ORDER.index(s) * 64
            two_at = PAIR_ORDER.index(s + 1) * 64
            value = acc[r, one_at : one_at + 64, 0:256] + acc[r, two_at : two_at + 64, 256:512]
            value = exact_right(value, to_natural)
            at = (r * 3 + s) * 64
            pack[at : at + 64, :] = value[:, 0:128]
            pack[576 + at : 640 + at, :] = value[:, 128:256]
    sums4 = exact_right(jnp.broadcast_to(sums4, (8, 256)), to_natural)
    pack[2992:2993, :] = sums4[0:1, 0:128]
    pack[2993:2994, :] = sums4[0:1, 128:256]

    begin2, count2 = start_of(2), count_of(2)

    def back_three(at):
        value = None
        for u in range(4):
            p, d = BACK_SOURCE[u]
            term = mm_nt(g4[p, slab(begin2 + 48 * d + at, 496), :], v4b[u])
            value = term if value is None else value + term
        here = slab(begin2 + at, 496)
        act = jnp.concatenate([x4[0, here, 0:128], x4[1, here, 0:128]], axis=1).astype(F32)
        t_g3[pl.ds(pl.multiple_of(8 + at, 8), 496), :] = (
            value * (1.0 - act * act) * kept(begin2 + at, 496)
        )

    blocks(count2, 496, back_three)
    for v in range(3):
        g3[begin2 : begin2 + count2, v * 256 : v * 256 + 256] = t_g3[7 + v : 7 + v + count2, :].astype(BF)

    value = inner(g3, 0, slice(256, 512))
    sums3 = jnp.sum(value.astype(F32), axis=0, keepdims=True)
    for r in range(3):
        term = mm_tn(inner(x3, r - 1, slice(0, 192)), value)
        term = exact_right(term, to_natural)
        at = 1152 + r * 192
        pack[at : at + 192, :] = term[:, 0:128]
        pack[576 + at : 768 + at, :] = term[:, 128:256]
    sums3 = exact_right(jnp.broadcast_to(sums3, (8, 256)), to_natural)
    pack[2994:2995, :] = sums3[0:1, 0:128]
    pack[2995:2996, :] = sums3[0:1, 128:256]

    begin1, count1 = start_of(1), count_of(1)

    def back_two(at):
        value = None
        for u in range(3):
            term = mm_nt(g3[slab(begin1 + 48 * (u - 1) + at, 448), :], v3b[u])
            value = term if value is None else value + term
        act = x3[slab(begin1 + at, 448), 64:128].astype(F32)
        t64[pl.ds(pl.multiple_of(8 + at, 8), 448), :] = (
            value * (1.0 - act * act) * kept(begin1 + at, 448)
        )

    blocks(count1, 448, back_two)
    three_shifts(g2, begin1, count1)

    value = inner(g2, 0, slice(64, 128))
    sums2 = jnp.sum(value.astype(F32), axis=0, keepdims=True)
    for r in range(3):
        at = 2304 + r * 192
        pack[at : at + 192, 0:64] = mm_tn(inner(x2, r - 1, slice(0, 192)), value)
    value = None
    for u in range(3):
        term = mm_nt(inner(g2, u - 1, slice(0, 192)), v2b[u])
        value = term if value is None else value + term
    act = inner(x2, 0, slice(64, 128)).astype(F32)
    value = (value * (1.0 - act * act)).astype(BF)
    sums1 = jnp.sum(value.astype(F32), axis=0, keepdims=True)
    pack[2996:2997, 0:64] = sums2
    pack[2996:2997, 64:128] = sums1
    term = mm_tn(inner(x1, 0, slice(0, 144)), value)
    for r in range(3):
        for s in range(3):
            at = 2880 + (r * 3 + s) * 12
            pack[at : at + 12, 0:64] = term[s * 48 + r * 16 : s * 48 + r * 16 + 12, :]
            pack[at : at + 12, 64:128] = jnp.zeros((12, 64), F32)


def compute_of(where_am_i, rows_in, cot_in, weights, biases):
    count3 = count_of(3) + 16
    scratch = (
        ((SPAN, 128), F32),
        ((SPAN, 144), F32),
        ((144, 448), F32),
        ((SPAN, 144), BF),
        ((count_of(5) + 16, 64), F32),
        ((SPAN, 192), BF),
        ((SPAN, 192), BF),
        ((count3, 256), F32),
        ((2, SPAN, 256), BF),
        ((4, count3, 256), F32),
        ((4, SPAN, 384), BF),
        ((3, 1152, 128), F32),
        ((SPAN, 432), F32),
        ((288, 1152), F32),
        ((SPAN, 432), BF),
        ((512, 192), BF),
        ((count3, 1024), F32),
        ((2, SPAN, 1024), BF),
        ((count_of(2) + 16, 256), F32),
        ((SPAN, 768), BF),
        ((SPAN, 192), BF),
        ((144, 64), BF),
        ((576, 256), BF),
        ((576, 256), BF),
        ((3, 256, 512), BF),
        ((4, 256, 1024), BF),
        ((3, 64, 768), BF),
        ((3, 64, 192), BF),
        ((6, 384, 192), BF),
        ((1024, 432), BF),
        ((3, 384, 512), F32),
        ((512, 192), F32),
        ((128, 768), F32),
        ((768, 128), F32),
        ((576, 432), F32),
    )
    vmem = pl.BlockSpec(memory_space=pltpu.VMEM)
    return pl.pallas_call(
        functools.partial(compute_kernel, where_am_i),
        out_shape=[
            jax.ShapeDtypeStruct((12, 64, 128), F32),
            jax.ShapeDtypeStruct((3072, 128), F32),
        ],
        in_specs=[vmem] * 12,
        out_specs=[vmem] * 2,
        scratch_shapes=[pltpu.VMEM(shape, kind) for shape, kind in scratch],
        compiler_params=pltpu.CompilerParams(vmem_limit_bytes=66000000),
        name="slab_compute",
    )(rows_in, cot_in, *weights, *biases)


def place():
    return lax.axis_index("gx"), lax.axis_index("gy")


def local(
    coarse,
    weight_one,
    weight_two,
    weight_three,
    weight_four,
    weight_five,
    bias_one,
    bias_two,
    bias_three,
    bias_four,
    bias_five,
    cotangent,
):
    row = jnp.pad(coarse.reshape(12, 512), ((0, 4), (0, 0)))
    rows_in, cot_in = gather_of(row, cotangent)
    weights = (
        weight_one.reshape(9, 12, 64),
        weight_two.reshape(576, 64),
        weight_three.reshape(576, 256),
        weight_four.reshape(576, 256),
        weight_five.reshape(576, 12),
    )
    biases = tuple(
        bias.reshape(1, -1) for bias in (bias_one, bias_two, bias_three, bias_four, bias_five)
    )
    fine, pack = compute_of(place, rows_in, cot_in, weights, biases)
    totals = totals_of(pack, float(16 * 128 * 512) ** -0.5)
    shapes = (
        weight_one.shape,
        weight_two.shape,
        weight_three.shape,
        weight_four.shape,
        weight_five.shape,
        (64,),
        (64,),
        (256,),
        (256,),
        (12,),
    )
    return (fine,) + tuple(total.reshape(shape) for total, shape in zip(totals, shapes))


def solution(mesh):
    in_specs = (
        P(None, ("gx", "gy"), None),
        P(),
        P(),
        P(),
        P(),
        P(),
        P(),
        P(),
        P(),
        P(),
        P(),
        P(None, "gx", "gy"),
    )
    out_specs = (P(None, "gx", "gy"), P(), P(), P(), P(), P(), P(), P(), P(), P(), P())
    return jax.shard_map(local, mesh=mesh, in_specs=in_specs, out_specs=out_specs, check_vma=False)
```

profile of v0, /device:TPU:1, one launch (start us, length us, event | category | flops | bytes accessed | tf_op | source)
XLA Modules:
  0.0 103.2 jit_solution(4747554635290053499)
XLA Ops:
  0.6 1.3 %pad.4.coarse = bf16[16,512]{1,0:T(8,128)(2,1)} pad(bf16[12,512]{1,0:T(8,128)(2,1)} %bitcast.31, bf16[]{:T(256)} %constant.2.clone.1), padding=0_4x0_0 | pad | bytes 28674 | tf_op jit(solution)/shard_map/jit(_pad)/pad | solution.py:941
  2.0 1.6 %copy.23 = bf16[3,3,64,12]{3,2,1,0:T(8,128)(2,1)} copy(bf16[3,3,64,12]{2,3,1,0:T(8,128)(2,1)} %param.17) | data formatting | bytes 27648 | tf_op args[5]
  3.5 21.7 %rim_gather.1 = (bf16[28,16,256]{2,1,0:T(8,128)(2,1)}, bf16[12,96,384]{2,1,0:T(8,128)(2,1)}) custom-call(bf16[16,512]{1,0:T(8,128)(2,1)} %pad.4.coarse, bf16[12,64,128]{2,1,0:T(8,128)(2,1)} %cot.1), custom_call_target="tpu_custom_call" | custom-call | tf_op jit(solution)/shard_map/rim_gather/pallas_call | solution.py:346
  25.3 32.4 %slab_compute.1 = (f32[12,64,128]{2,1,0:T(8,128)}, f32[3072,128]{1,0:T(8,128)}) custom-call(bf16[28,16,256]{2,1,0:T(8,128)(2,1)} %get-tuple-element.25.rows_in, bf16[12,96,384]{2,1,0:T(8,128)(2,1)} %get-tuple-element.26.cot_in, bf16[9,12,64]{2,1,0:T(8,128)(2,1)} %bitcast.30, bf16[576,64]{1,0:T(8,128)(2,1)} %bitcast.28, bf16[576,256]{1,0:T(8,128)(2,1)} %bitcast.24, ...), custom_call_target="tpu_custom_call" | custom-call | tf_op jit(solution)/shard_map/slab_compute/pallas_call | solution.py:909
  57.7 35.0 %grad_totals.1 = (f32[9,12,64]{2,1,0:T(8,128)}, f32[576,64]{1,0:T(8,128)}, f32[576,256]{1,0:T(8,128)}, f32[576,256]{1,0:T(8,128)}, f32[576,12]{1,0:T(8,128)}, /*...) custom-call(f32[3072,128]{1,0:T(8,128)} %get-tuple-element.28.pack), custom_call_target="tpu_custom_call" | custom-call | tf_op jit(solution)/shard_map/grad_totals/pallas_call | solution.py:224
  92.7 0.0 copy-start
  92.7 1.8 %copy.24 = f32[3,3,64,12]{2,3,1,0:T(8,128)} copy(f32[3,3,64,12]{3,2,1,0:T(8,128)} %bitcast.27) | data formatting | bytes 55296
  94.5 0.0 copy-start.5
  94.6 0.0 copy-start.3
  94.6 1.5 %copy.34 = f32[3,3,12,64]{3,2,1,0:T(8,128)} copy(f32[3,3,12,64]{3,2,1,0:T(8,128)} %bitcast.29) | data formatting | bytes 55296
  96.1 1.7 %copy.35 = f32[3,3,64,64]{3,2,1,0:T(8,128)} copy(f32[3,3,64,64]{3,2,1,0:T(8,128)} %bitcast.26) | data formatting | bytes 294912
  97.8 1.9 %copy.36 = f32[3,3,64,256]{3,2,1,0:T(8,128)} copy(f32[3,3,64,256]{3,2,1,0:T(8,128)} %bitcast.23) | data formatting | bytes 1179648
  99.7 0.0 copy-done
  99.7 0.8 copy.37
  100.5 0.0 copy-done.5
  100.5 0.5 copy.38
  101.0 0.0 copy-done.4
  101.0 0.5 copy.39
  101.6 0.0 copy-done.2
  101.6 0.6 copy.40
  102.1 0.0 copy-done.1
  102.1 0.6 copy.41
  102.7 0.0 copy-done.3
  102.7 0.5 copy.42
  (3 shorter events, 0.0 us)
Async XLA Ops:
  92.7 7.0 %copy-start = (f32[576,256]{1,0:T(8,128)S(1)}, f32[576,256]{1,0:T(8,128)}, u32[]{:S(2)}) copy-start(f32[576,256]{1,0:T(8,128)} %get-tuple-element.32) | copy-start | bytes 1769476
  94.5 6.0 %copy-start.5 = (f32[1,64]{1,0:T(1,128)S(1)}, f32[1,64]{1,0:T(1,128)}, u32[]{:S(2)}) copy-start(f32[1,64]{1,0:T(1,128)} %get-tuple-element.34) | copy-start | bytes 772
  94.6 6.5 %copy-start.4 = (f32[1,64]{1,0:T(1,128)S(1)}, f32[1,64]{1,0:T(1,128)}, u32[]{:S(2)}) copy-start(f32[1,64]{1,0:T(1,128)} %get-tuple-element.35) | copy-start | bytes 772
  94.6 7.0 %copy-start.2 = (f32[1,256]{1,0:T(1,128)S(1)}, f32[1,256]{1,0:T(1,128)}, u32[]{:S(2)}) copy-start(f32[1,256]{1,0:T(1,128)} %get-tuple-element.36) | copy-start | bytes 3076
  94.6 7.6 %copy-start.1 = (f32[1,256]{1,0:T(1,128)S(1)}, f32[1,256]{1,0:T(1,128)}, u32[]{:S(2)}) copy-start(f32[1,256]{1,0:T(1,128)} %get-tuple-element.37) | copy-start | bytes 3076
  94.6 8.1 %copy-start.3 = (f32[1,12]{1,0:T(1,128)S(1)}, f32[1,12]{1,0:T(1,128)}, u32[]{:S(2)}) copy-start(f32[1,12]{1,0:T(1,128)} %get-tuple-element.38) | copy-start | bytes 148
where the time goes:
time: 104 us; the launch traced here: 103 us
  Pallas kernels  89.2 us (86%)
  local copies, waits for them, and re-layouts  13.3 us (13%)
    pallas_call x1, Pallas kernels, totals_of(): pl.pallas_call(functools.partial(total_kernel, scale), out_shape=[jax.Sha...  35 us
    pallas_call x1, Pallas kernels, compute_of(): pl.pallas_call(functools.partial(compute_kernel, where_am_i), out_shape=[...  32.4 us
    pallas_call x1, Pallas kernels, gather_of(): pl.pallas_call(gather_kernel, out_shape=[jax.ShapeDtypeStruct((28, 16, 25...  21.7 us
    unnamed x23, local copies, waits for them, and re-layouts  12 us

commit v1 on v0

v1 whole, which is shorter than its diff:
```python
import functools

import jax
import jax.numpy as jnp
from jax import lax
from jax.experimental import pallas as pl
from jax.experimental.pallas import tpu as pltpu
from jax.sharding import PartitionSpec as P

MESH_ID = pl.DeviceIdType.MESH


def coordinates():
    gx = lax.axis_index("gx")
    gy = lax.axis_index("gy")
    return (gx % 4, (gy // 2) % 4, (gx // 4) * 2 + gy // 8), gy % 2


def device_at(place, core):
    x, y, z = place
    return ((z // 2) * 4 + x, (z % 2) * 8 + y * 2 + core)


def along(place, axis, step):
    moved = list(place)
    moved[axis] = (place[axis] + step) % 4
    return moved


def rows_at(start, count):
    return pl.ds(pl.multiple_of(start, 8), count)


FLOWS = (
    (0, 512, (0, 1, 2)),
    (512, 512, (1, 2, 0)),
    (1024, 256, (2, 0, 1)),
    (1280, 512, (1, 2, 0)),
    (1792, 512, (2, 0, 1)),
    (2304, 256, (0, 1, 2)),
    (2560, 256, (0, 1, 2)),
    (2816, 256, (1, 2, 0)),
)
WHEN_READY = (0, 0, 0, 2, 2, 2, 3, 3)


class Flow:
    def __init__(self, number, place, core, pack, whole, base, rows, order):
        self.number, self.place, self.core = number, place, core
        self.pack, self.whole = pack, whole
        self.base, self.order = base, order
        self.sizes = (rows // 2, rows // 8, rows // 32)
        self.sent = []
        self.now = []

    def send(self, src, dst, sem, index, peer):
        copy = pltpu.make_async_remote_copy(
            src_ref=src,
            dst_ref=dst,
            send_sem=self.sems[sem].at[index],
            recv_sem=self.sems[sem + 1].at[index],
            device_id=peer,
            device_id_type=MESH_ID,
        )
        copy.start()
        self.sent.append(copy)
        self.now.append(copy)

    def arrive(self):
        for copy in self.now:
            copy.wait_recv()
        self.now = []

    def to_partner(self, src, dst, index):
        self.send(src, dst, 0, (self.number, index), device_at(self.place, 1 - self.core))

    def to_axis(self, turn, hop, views):
        axis = self.order[turn]
        for step in (1, 2, 3):
            src, dst = views(axis, step)
            self.send(
                src,
                dst,
                2,
                (self.number, hop, step - 1),
                device_at(along(self.place, axis, step), self.core),
            )

    def row(self, level):
        row = self.base + self.core * self.sizes[0]
        for turn in range(level):
            row = row + self.place[self.order[turn]] * self.sizes[turn + 1]
        return row

    def advance(self, stage):
        pair_in, pair_sum, in_a, sum_a, in_b, sum_b, in_c = self.refs
        half, fourth, small = self.sizes
        two, eight, many = self.base // 2, self.base // 8, self.base // 32
        if stage == 0:
            self.to_partner(
                self.pack.at[rows_at(self.base + (1 - self.core) * half, half)],
                pair_in.at[pl.ds(two, half)],
                0,
            )
            return
        self.arrive()
        if stage == 1:
            own = self.pack[rows_at(self.base + self.core * half, half), :]
            pair_sum[pl.ds(two, half), :] = own + pair_in[pl.ds(two, half), :]
            self.to_axis(
                0,
                0,
                lambda axis, step: (
                    pair_sum.at[rows_at(two + (self.place[axis] + step) % 4 * fourth, fourth)],
                    in_a.at[step - 1, pl.ds(eight, fourth)],
                ),
            )
        elif stage == 2:
            value = pair_sum[rows_at(two + self.place[self.order[0]] * fourth, fourth), :]
            for step in range(3):
                value = value + in_a[step, pl.ds(eight, fourth), :]
            sum_a[pl.ds(eight, fourth), :] = value
            self.to_axis(
                1,
                1,
                lambda axis, step: (
                    sum_a.at[rows_at(eight + (self.place[axis] + step) % 4 * small, small)],
                    in_b.at[step - 1, pl.ds(many, small)],
                ),
            )
        elif stage == 3:
            value = sum_a[rows_at(eight + self.place[self.order[1]] * small, small), :]
            for step in range(3):
                value = value + in_b[step, pl.ds(many, small), :]
            in_c[0, pl.ds(many, small), :] = value
            self.to_axis(
                2,
                2,
                lambda axis, step: (
                    in_c.at[0, pl.ds(many, small)],
                    in_c.at[step, pl.ds(many, small)],
                ),
            )
        elif stage == 4:
            here = self.place[self.order[2]]
            terms = [in_c[(here - other + 4) % 4, pl.ds(many, small), :] for other in range(4)]
            self.whole[rows_at(self.row(2), small), :] = (terms[0] + terms[1]) + (
                terms[2] + terms[3]
            )
            block = self.whole.at[rows_at(self.row(2), small)]
            self.to_axis(1, 3, lambda axis, step: (block, block))
        elif stage == 5:
            block = self.whole.at[rows_at(self.row(1), fourth)]
            self.to_axis(0, 4, lambda axis, step: (block, block))
        elif stage == 6:
            block = self.whole.at[rows_at(self.row(0), half)]
            self.to_partner(block, block, 1)

    def drain(self):
        for copy in self.sent:
            copy.wait_send()


def window(gy):
    return pl.multiple_of(jnp.clip(jnp.right_shift(gy * 32 - 8, 7), 0, 2) * 128, 128)


STRIDE = 48
ROWS = 30
SPAN = ROWS * STRIDE
BF = jnp.bfloat16
F32 = jnp.float32


def start_of(halo):
    return (7 - halo) * STRIDE - 16


def count_of(halo):
    return (16 + 2 * halo) * STRIDE + 32


def mm(lhs, rhs):
    return lax.dot_general(lhs, rhs, (((1,), (0,)), ((), ())), preferred_element_type=F32)


def mm_nt(lhs, rhs):
    return lax.dot_general(lhs, rhs, (((1,), (1,)), ((), ())), preferred_element_type=F32)


def mm_tn(lhs, rhs):
    return lax.dot_general(lhs, rhs, (((0,), (0,)), ((), ())), preferred_element_type=F32)


def iota(shape, dim):
    return lax.broadcasted_iota(jnp.int32, shape, dim)


def over(value, divisor):
    return lax.shift_right_logical(value * ((1 << 16) // divisor + 1), 16)


def one_hot(flag):
    return jnp.where(flag, 1.0, 0.0).astype(F32).astype(BF)


def three_parts(value):
    high = value.astype(BF)
    rest = value - high.astype(F32)
    middle = rest.astype(BF)
    return high, middle, (rest - middle.astype(F32)).astype(BF)


def exact_right(value, selector):
    parts = three_parts(value)
    return (mm(parts[2], selector) + mm(parts[1], selector)) + mm(parts[0], selector)


def blocks(total, chunk, body):
    def step(index, carry):
        body(pl.multiple_of(index * chunk, 16))
        return carry

    lax.fori_loop(0, total // chunk, step, 0)


def slab(start, count):
    if isinstance(start, int):
        return pl.ds(start, count)
    return pl.ds(pl.multiple_of(start, 16), count)


def inner(ref, shift, lanes):
    first = 7 + shift
    picked = [ref[(first + row) * STRIDE : (first + row) * STRIDE + 32, lanes] for row in range(16)]
    return jnp.concatenate(picked, axis=0)


ROW_SOURCE = (((1, -1), (0, 0), (1, 0)), ((0, 0), (1, 0), (0, 1)))
BACK_SOURCE = ((1, -1), (0, 0), (1, 0), (0, 1))
FINE_SOURCE = ((3, -1), (0, 0), (1, 0), (2, 0), (3, 0), (0, 1))
PAIR_ORDER = (1, 2, 3, 0)
FINE_ORDER = (1, 2, 3, 4, 5, 0)


def train_kernel(
    coarse,
    cot,
    w1,
    w2,
    w3,
    w4,
    w5,
    b1,
    b2,
    b3,
    b4,
    b5,
    fine,
    whole,
    rows_in,
    cot_in,
    known,
    pack,
    mask,
    t_c1,
    m_c1,
    x1,
    t64,
    x2,
    x3,
    t3,
    x4,
    t4,
    x5,
    ay,
    t_cot,
    m_cot,
    xc,
    g5,
    t_g4,
    g4,
    t_g3,
    g3,
    g2,
    v1,
    v3,
    v4,
    v4f,
    v4b,
    v3b,
    v2b,
    v5f,
    v5b,
    acc,
    z5,
    turned,
    lined,
    wide,
    pair_in,
    pair_sum,
    in_a,
    sum_a,
    in_b,
    sum_b,
    in_c,
    keep_sem,
    row_send,
    row_recv,
    far_send,
    far_recv,
    cot_send,
    cot_recv,
    pair_send,
    pair_recv,
    hop_send,
    hop_recv,
):
    gx = lax.axis_index("gx")
    gy = lax.axis_index("gy")

    def peer(step_x, step_y):
        return ((gx + step_x + 8) % 8, (gy + step_y + 16) % 16)

    barrier = pltpu.get_barrier_semaphore()
    for step_x in (-1, 0, 1):
        for step_y in range(16):
            if step_x != 0 or step_y != 0:
                pl.semaphore_signal(
                    barrier, inc=1, device_id=peer(step_x, step_y), device_id_type=MESH_ID
                )
    spot_now, core = coordinates()
    partner = device_at(spot_now, 1 - core)
    for axis in range(3):
        for step in (1, 2, 3):
            pl.semaphore_signal(
                barrier,
                inc=1,
                device_id=device_at(along(spot_now, axis, step), core),
                device_id_type=MESH_ID,
            )
    locals_ = [
        pltpu.make_async_copy(
            cot, cot_in.at[1, :, pl.ds(16, 64), :], keep_sem.at[0]
        ),
        pltpu.make_async_copy(
            coarse.at[:, pl.ds(window(gy), 256)], rows_in.at[6 + gy], keep_sem.at[1]
        ),
    ]
    for copy in locals_:
        copy.start()
    pl.semaphore_wait(barrier, 56)

    def remote(src, dst, send_sem, recv_sem, target):
        return pltpu.make_async_remote_copy(
            src_ref=src,
            dst_ref=dst,
            send_sem=send_sem,
            recv_sem=recv_sem,
            device_id=target,
            device_id_type=MESH_ID,
        )

    def row_copy(step, dst_row, send_sem, recv_sem, step_x):
        target = peer(step_x, step)
        return remote(
            coarse.at[:, pl.ds(window(target[1]), 256)],
            rows_in.at[dst_row],
            send_sem,
            recv_sem,
            target,
        )

    copies = []
    parts = ((16, 48, 0), (64, 0, 16), (16, 0, 80))
    for index_x, step_x in enumerate((1, 0, -1)):
        count, src_row, dst_row = parts[index_x]
        for index_y, step_y in enumerate((1, 0, -1)):
            if step_x == 0 and step_y == 0:
                continue
            copies.append(
                remote(
                    cot.at[:, pl.ds(src_row, count), :],
                    cot_in.at[index_y, :, pl.ds(dst_row, count), :],
                    cot_send.at[index_x, index_y],
                    cot_recv.at[index_x, index_y],
                    peer(step_x, step_y),
                )
            )
    for step in range(1, 16):
        copies.append(row_copy(step, 6 + gy, row_send.at[step], row_recv.at[step], 0))
    for copy in copies:
        copy.start()

    def far(step_x, dst_row, slot):
        return [
            row_copy(step, dst_row, far_send.at[step], far_recv.at[slot], step_x)
            for step in range(16)
        ]

    @pl.when(gy < 6)
    def _():
        for copy in far(-1, 22 + gy, 6 + gy):
            copy.start()

    @pl.when(gy >= 10)
    def _():
        for copy in far(1, gy - 10, gy - 10):
            copy.start()

    def await_rows():
        locals_[1].wait()
        for step in range(1, 16):
            row_copy(
                step, 6 + (gy - step + 16) % 16, row_send.at[step], row_recv.at[step], 0
            ).wait_recv()
        for slot in range(12):
            dst_row = slot if slot < 6 else 16 + slot
            row_copy(1, dst_row, far_send.at[0], far_recv.at[slot], 0).wait_recv()

    def await_cot():
        locals_[0].wait()
        for copy in copies[:8]:
            copy.wait_recv()

    def drain_gather():
        for copy in copies:
            copy.wait_send()

        @pl.when(gy < 6)
        def _():
            for copy in far(-1, 22 + gy, 6 + gy):
                copy.wait_send()

        @pl.when(gy >= 10)
        def _():
            for copy in far(1, gy - 10, gy - 10):
                copy.wait_send()


    flows = [
        Flow(number, spot_now, core, pack, whole, *FLOWS[number])
        for number in range(len(FLOWS))
    ]
    refs = (pair_in, pair_sum, in_a, sum_a, in_b, sum_b, in_c)
    sems = (pair_send, pair_recv, hop_send, hop_recv)
    for flow in flows:
        flow.refs = refs
        flow.sems = sems

    def progress(point):
        for number, flow in enumerate(flows):
            stage = point - WHEN_READY[number]
            if 0 <= stage < 8:
                flow.advance(stage)

    base_row = gx * 16
    base_col = gy * 32

    place = iota((SPAN, 128), 0)
    line = over(place, STRIDE)
    col = place - line * STRIDE
    left = jnp.where(col >= 40, 1, 0)
    row = line - 7 + left + base_row
    col = col - left * STRIDE + base_col
    ok = (row >= 0) & (row < 128) & (col >= 0) & (col < 512)
    mask[...] = jnp.where(ok, 1.0, 0.0)

    def kept(start, count):
        return mask[slab(start, count), 0:1]

    lane = iota((256, 256), 1)
    natural = iota((256, 256), 0)
    wanted = (lane - over(lane, 64) * 64) * 4 + over(lane, 64)
    to_phase = one_hot(natural == wanted)
    wanted_back = (natural - over(natural, 64) * 64) * 4 + over(natural, 64)
    to_natural = one_hot(lane == wanted_back)
    v3[...] = mm(w3[...], to_phase).astype(BF)
    v4[...] = mm(w4[...], to_phase).astype(BF)
    bias3 = exact_right(jnp.broadcast_to(b3[...], (8, 256)), to_phase)[0:1]
    bias4 = exact_right(jnp.broadcast_to(b4[...], (8, 256)), to_phase)[0:1]

    v1[...] = jnp.zeros(v1.shape, BF)
    for r in range(3):
        for s in range(3):
            v1[s * 48 + r * 16 : s * 48 + r * 16 + 12, :] = w1[r * 3 + s]
    for r in range(3):
        for position, c4 in enumerate(PAIR_ORDER):
            for q in range(2):
                s = c4 - q
                target = (slice(position * 64, position * 64 + 64), slice(q * 256, q * 256 + 256))
                if 0 <= s <= 2:
                    v4f[r, target[0], target[1]] = v4[(r * 3 + s) * 64 : (r * 3 + s) * 64 + 64, :]
                else:
                    v4f[r, target[0], target[1]] = jnp.zeros((64, 256), BF)
    for u in range(4):
        for a in range(2):
            for b in range(2):
                for position, v in enumerate(PAIR_ORDER):
                    r, s = a + 2 - u, b + 2 - v
                    at = (slice((2 * a + b) * 64, (2 * a + b) * 64 + 64),)
                    at = at + (slice(position * 256, position * 256 + 256),)
                    if 0 <= r <= 2 and 0 <= s <= 2:
                        tap = (r * 3 + s) * 64
                        v4b[u, at[0], at[1]] = v4[tap : tap + 64, :]
                    else:
                        v4b[u, at[0], at[1]] = jnp.zeros((64, 256), BF)
    for u in range(3):
        for v in range(3):
            tap = ((2 - u) * 3 + 2 - v) * 64
            v3b[u, :, v * 256 : v * 256 + 256] = v3[tap : tap + 64, :]
            v2b[u, :, v * 64 : v * 64 + 64] = w2[tap : tap + 64, :]

    def spread_out(width, group):
        lanes = iota((12, width), 1)
        spread = one_hot((lanes - over(lanes, group) * group) == iota((12, width), 0))
        for tap in range(9):
            wide[tap * 64 : tap * 64 + 64, 0:width] = mm_tn(w5[tap], spread)

    spread_out(256, 16)
    lanes5 = iota((64, 256), 1)
    cell5 = over(lanes5, 16)
    col5 = over(cell5, 4)
    row5 = cell5 - col5 * 4
    for t in range(6):
        for position, v in enumerate(FINE_ORDER):
            value = jnp.zeros((64, 256), F32)
            for r in range(max(0, t - 3), min(2, t) + 1):
                for s in range(max(0, v - 3), min(2, v) + 1):
                    tap = (r * 3 + s) * 64
                    value = jnp.where(
                        (row5 == t - r) & (col5 == v - s), wide[tap : tap + 64, 0:256], value
                    )
            v5f[t, position * 64 : position * 64 + 64, :] = value.astype(BF)
    spread_out(432, 12)
    lanes6 = iota((64, 432), 1)
    cell6 = over(lanes6, 12)
    col6 = over(cell6, 6)
    row6 = cell6 - col6 * 6
    for big_r in range(4):
        for big_c in range(4):
            value = jnp.zeros((64, 432), F32)
            for r in range(3):
                for s in range(3):
                    tap = (r * 3 + s) * 64
                    value = jnp.where(
                        (row6 == big_r + 2 - r) & (col6 == big_c + 2 - s),
                        wide[tap : tap + 64, :],
                        value,
                    )
            at = (big_r * 4 + big_c) * 64
            v5b[at : at + 64, :] = value.astype(BF)

    t64[0:8, :] = jnp.zeros((8, 64), F32)
    for ref in (t3, t4, t_g3, t_g4):
        for tile in range(ref.shape[0]):
            ref[tile, 0:8, :] = jnp.zeros((8, 128), F32)
            ref[tile, ref.shape[1] - 8 :, :] = jnp.zeros((8, 128), F32)
    begin, count = start_of(3), count_of(3)
    for a in range(2):
        x4[a, begin - 48 : begin, :] = jnp.zeros((48, 256), BF)
        x4[a, begin + count : begin + count + 48, :] = jnp.zeros((48, 256), BF)

    t_c1[...] = jnp.zeros(t_c1.shape, F32)
    t_cot[...] = jnp.zeros(t_cot.shape, F32)
    known[...] = jnp.zeros(known.shape, F32)
    for first, last in ((1152, 1280), (2432, 2560), (2816, 3072)):
        pack[first:last, :] = jnp.zeros((last - first, 128), F32)

    spot = iota((144, 256), 0)
    tap_col = over(spot, 48)
    want = spot - tap_col * 48 - 8 + tap_col - 1 + base_col
    first = jnp.clip(jnp.right_shift(base_col - 8, 7), 0, 2) * 128
    pick = one_hot((want == iota((144, 256), 1) + first) & (want >= 0) & (want < 512))
    await_rows()
    for k in range(28):
        present = (base_row - 6 + k >= 0) & (base_row - 6 + k < 128)
        known[k * 16 : k * 16 + 12, :] = jnp.where(present, rows_in[k].astype(F32), 0.0)
    m_c1[...] = mm_nt(pick, known[...].astype(BF))
    for i in range(-5, 21):
        for s in range(3):
            at = (i + 7) * STRIDE - 8
            t_c1[at : at + 48, s * 48 : s * 48 + 48] = m_c1[
                s * 48 : s * 48 + 48, (i + 5) * 16 : (i + 5) * 16 + 48
            ]
    x1[...] = t_c1[...].astype(BF)

    def three_shifts(target, begin, count):
        t64[8 + count : 16 + count, :] = jnp.zeros((8, 64), F32)
        for s in range(3):
            target[begin : begin + count, s * 64 : s * 64 + 64] = t64[7 + s : 7 + s + count, :].astype(BF)

    begin, count = start_of(5), count_of(5)

    def one(at):
        z = mm(x1[slab(begin + at, 256), :], v1[...]) + b1[...]
        t64[pl.ds(pl.multiple_of(8 + at, 8), 256), :] = (
            jnp.tanh(z) * kept(begin + at, 256)
        )

    blocks(count, 256, one)
    three_shifts(x2, begin, count)

    begin2, count2 = start_of(4), count_of(4)

    def two(at):
        z = b2[...]
        for r in range(3):
            z = z + mm(x2[slab(begin2 + 48 * (r - 1) + at, 592), :], w2[192 * r : 192 * r + 192, :])
        t64[pl.ds(pl.multiple_of(8 + at, 8), 592), :] = jnp.tanh(z) * kept(begin2 + at, 592)

    blocks(count2, 592, two)
    three_shifts(x3, begin2, count2)

    begin3, count3 = start_of(3), count_of(3)

    def three(at):
        z = bias3
        for r in range(3):
            z = z + mm(x3[slab(begin3 + 48 * (r - 1) + at, 272), :], v3[192 * r : 192 * r + 192, :])
        z = jnp.tanh(z) * kept(begin3 + at, 272)
        for a in range(2):
            t3[a, pl.ds(pl.multiple_of(8 + at, 8), 272), :] = z[:, a * 128 : a * 128 + 128]

    blocks(count3, 272, three)
    for a in range(2):
        at = slice(begin3, begin3 + count3)
        x4[a, at, 0:128] = t3[a, 8 : 8 + count3, :].astype(BF)
        x4[a, at, 128:192] = t3[a, 9 : 9 + count3, 0:64].astype(BF)
        x4[a, at, 192:256] = t3[a, 7 : 7 + count3, 64:128].astype(BF)

    def four(at):
        for p in range(2):
            z = jnp.concatenate([bias4, bias4], axis=1)
            for r in range(3):
                a, d = ROW_SOURCE[p][r]
                z = z + mm(x4[a, slab(begin3 + 48 * d + at, 272), :], v4f[r])
            z = jnp.tanh(z) * kept(begin3 + at, 272)
            for half in range(2):
                for q in range(2):
                    t4[4 * p + 2 * half + q, pl.ds(pl.multiple_of(8 + at, 8), 272), :] = z[
                        :, q * 256 + half * 128 : q * 256 + half * 128 + 128
                    ]

    blocks(count3, 272, four)
    for big_r in range(4):
        at = slice(begin3, begin3 + count3)
        x5[big_r, at, 0:128] = t4[2 * big_r, 8 : 8 + count3, :].astype(BF)
        x5[big_r, at, 128:256] = t4[2 * big_r + 1, 8 : 8 + count3, :].astype(BF)
        x5[big_r, at, 256:320] = t4[2 * big_r, 9 : 9 + count3, 0:64].astype(BF)
        x5[big_r, at, 320:384] = t4[2 * big_r + 1, 7 : 7 + count3, 64:128].astype(BF)

    await_cot()
    fine_row = iota((96, 128), 0) - 16 + gx * 64
    row_ok = (fine_row >= 0) & (fine_row < 512)
    for o in range(12):
        for third in range(3):
            value = cot_in[third, o].astype(F32)
            ay[third, pl.ds(o, 96, stride=12), :] = jnp.where(row_ok, value, 0.0)
    spot = iota((288, 384), 0)
    tap_col = over(spot, 48)
    want = (spot - tap_col * 48 - 8) * 4 + tap_col - 1
    real = want + gy * 128
    pick = one_hot((iota((288, 384), 1) == want + 128) & (real >= 0) & (real < 2048))
    value = None
    for third in range(3):
        term = mm_nt(pick[:, third * 128 : third * 128 + 128], ay[third].astype(BF))
        value = term if value is None else value + term
    m_cot[...] = value
    for i in range(-3, 19):
        for v in range(6):
            at = (i + 7) * STRIDE - 8
            t_cot[at : at + 48, v * 72 : v * 72 + 72] = m_cot[
                v * 48 : v * 48 + 48, (4 * i + 15) * 12 : (4 * i + 15) * 12 + 72
            ]
    xc[...] = t_cot[...].astype(BF)
    for big_c in range(4):
        at = (big_c + 1) * 72 + 12
        g5[:, big_c * 48 : big_c * 48 + 48] = inner(t_cot, 0, slice(at, at + 48)).astype(BF)

    lanes5 = iota((384, 192), 1)
    cell5 = over(lanes5, 12)
    col5 = over(cell5, 4)
    row5 = cell5 - col5 * 4
    for r in range(3):
        acc[r, 0:384, 0:192] = jnp.zeros((384, 192), F32)
    for t in range(6):
        big_r, d = FINE_SOURCE[t]
        z5[0:384, 0:192] = mm_tn(inner(x5.at[big_r], d, slice(0, 384)), g5[...])
        for r in range(max(0, t - 3), min(2, t) + 1):
            acc[r, 0:384, 0:192] = jnp.where(row5 == t - r, z5[0:384, 0:192], acc[r, 0:384, 0:192])
    fold_lane = iota((16, 192), 1)
    fold = one_hot((fold_lane - over(fold_lane, 12) * 12) == iota((16, 192), 0))
    col5 = col5[0:64]
    for r in range(3):
        for s in range(3):
            value = jnp.zeros((64, 192), F32)
            for big_c in range(4):
                position = FINE_ORDER.index(big_c + s)
                value = jnp.where(
                    col5 == big_c, acc[r, position * 64 : position * 64 + 64, 0:192], value
                )
            tap = r * 3 + s
            parts = three_parts(value)
            value = (mm_nt(fold, parts[2]) + mm_nt(fold, parts[1])) + mm_nt(fold, parts[0])
            at = 1152 + 16 * (tap // 2)
            pack[at : at + 16, 64 * (tap % 2) : 64 * (tap % 2) + 64] = value
    sums5 = jnp.sum(g5[...].astype(F32), axis=0, keepdims=True)
    fold_lane = iota((192, 128), 0)
    fold = one_hot((fold_lane - over(fold_lane, 12) * 12) == iota((192, 128), 1))
    pack[1234:1235, :] = exact_right(jnp.broadcast_to(sums5, (8, 192)), fold)[0:1]

    def back_four(at):
        here = slab(begin3 + at, 272)
        keep = kept(begin3 + at, 272)
        for big_r in range(4):
            value = mm_nt(xc[here, :], v5b[big_r * 256 : big_r * 256 + 256, :])
            act = x5[big_r, here, 0:256].astype(F32)
            value = value * (1.0 - act * act) * keep
            for q in range(2):
                t_g4[2 * big_r + q, pl.ds(pl.multiple_of(8 + at, 8), 272), :] = value[
                    :, q * 128 : q * 128 + 128
                ]

    blocks(count3, 272, back_four)
    for p in range(2):
        at = slice(begin3, begin3 + count3)
        for half in range(2):
            src = (2 * p + half) * 2
            dst = half * 128
            for q in range(2):
                g4[p, at, q * 256 + dst : q * 256 + dst + 128] = t_g4[
                    src + q, 8 : 8 + count3, :
                ].astype(BF)
            g4[p, at, 512 + dst : 640 + dst] = t_g4[src, 9 : 9 + count3, :].astype(BF)
            g4[p, at, 768 + dst : 896 + dst] = t_g4[src + 1, 7 : 7 + count3, :].astype(BF)

    sums4 = jnp.zeros((1, 256), F32)
    for p in range(2):
        value = inner(g4.at[p], 0, slice(0, 512))
        sums = jnp.sum(value.astype(F32), axis=0, keepdims=True)
        sums4 = sums4 + sums[:, 0:256] + sums[:, 256:512]
        for r in range(3):
            a, d = ROW_SOURCE[p][r]
            term = mm_tn(inner(x4.at[a], d, slice(0, 256)), value)
            if p == 0:
                acc[r, 0:256, :] = term
            else:
                acc[r, 0:256, :] = acc[r, 0:256, :] + term
    for r in range(3):
        for s in range(3):
            one_at = PAIR_ORDER.index(s) * 64
            two_at = PAIR_ORDER.index(s + 1) * 64
            value = acc[r, one_at : one_at + 64, 0:256] + acc[r, two_at : two_at + 64, 256:512]
            value = exact_right(value, to_natural)
            at = (r * 3 + s) * 64
            pack[at : at + 64, :] = value[:, 0:128]
            pack[576 + at : 640 + at, :] = value[:, 128:256]
    sums4 = exact_right(jnp.broadcast_to(sums4, (8, 256)), to_natural)
    pack[1232:1233, :] = sums4[0:1, 0:128]
    pack[1233:1234, :] = sums4[0:1, 128:256]

    progress(0)

    begin2, count2 = start_of(2), count_of(2)

    def back_three(at):
        value = None
        for u in range(4):
            p, d = BACK_SOURCE[u]
            term = mm_nt(g4[p, slab(begin2 + 48 * d + at, 496), :], v4b[u])
            value = term if value is None else value + term
        here = slab(begin2 + at, 496)
        act = jnp.concatenate([x4[0, here, 0:128], x4[1, here, 0:128]], axis=1).astype(F32)
        value = value * (1.0 - act * act) * kept(begin2 + at, 496)
        for a in range(2):
            t_g3[a, pl.ds(pl.multiple_of(8 + at, 8), 496), :] = value[:, a * 128 : a * 128 + 128]

    blocks(count2, 496, back_three)
    for v in range(3):
        for a in range(2):
            at = v * 256 + a * 128
            g3[begin2 : begin2 + count2, at : at + 128] = t_g3[a, 7 + v : 7 + v + count2, :].astype(BF)

    progress(1)

    value = inner(g3, 0, slice(256, 512))
    sums3 = jnp.sum(value.astype(F32), axis=0, keepdims=True)
    for r in range(3):
        term = mm_tn(inner(x3, r - 1, slice(0, 192)), value)
        term = exact_right(term, to_natural)
        at = 1280 + r * 192
        pack[at : at + 192, :] = term[:, 0:128]
        pack[576 + at : 768 + at, :] = term[:, 128:256]
    sums3 = exact_right(jnp.broadcast_to(sums3, (8, 256)), to_natural)
    pack[2432:2433, :] = sums3[0:1, 0:128]
    pack[2433:2434, :] = sums3[0:1, 128:256]

    progress(2)

    begin1, count1 = start_of(1), count_of(1)

    def back_two(at):
        value = None
        for u in range(3):
            term = mm_nt(g3[slab(begin1 + 48 * (u - 1) + at, 448), :], v3b[u])
            value = term if value is None else value + term
        act = x3[slab(begin1 + at, 448), 64:128].astype(F32)
        t64[pl.ds(pl.multiple_of(8 + at, 8), 448), :] = (
            value * (1.0 - act * act) * kept(begin1 + at, 448)
        )

    blocks(count1, 448, back_two)
    three_shifts(g2, begin1, count1)

    value = inner(g2, 0, slice(64, 128))
    sums2 = jnp.sum(value.astype(F32), axis=0, keepdims=True)
    for r in range(3):
        term = mm_tn(inner(x2, r - 1, slice(0, 192)), value)
        for s in range(3):
            tap = r * 3 + s
            at = 2560 + 64 * (tap // 2)
            pack[at : at + 64, 64 * (tap % 2) : 64 * (tap % 2) + 64] = term[s * 64 : s * 64 + 64, :]
    value = None
    for u in range(3):
        term = mm_nt(inner(g2, u - 1, slice(0, 192)), v2b[u])
        value = term if value is None else value + term
    act = inner(x2, 0, slice(64, 128)).astype(F32)
    value = (value * (1.0 - act * act)).astype(BF)
    sums1 = jnp.sum(value.astype(F32), axis=0, keepdims=True)
    pack[2960:2961, 0:64] = sums2
    pack[2960:2961, 64:128] = sums1
    term = mm_tn(inner(x1, 0, slice(0, 144)), value)
    for r in range(3):
        for s in range(3):
            tap = r * 3 + s
            at = 2880 + 16 * (tap // 2)
            pack[at : at + 16, 64 * (tap % 2) : 64 * (tap % 2) + 64] = term[
                s * 48 + r * 16 : s * 48 + r * 16 + 16, :
            ]
    progress(3)

    z = jnp.zeros((512, 256), F32)
    for t in range(6):
        big_r, d = FINE_SOURCE[t]
        z = z + mm(inner(x5.at[big_r], d, slice(0, 384)), v5f[t])
    z5[...] = z
    progress(4)
    for i in range(16):
        for big_c in range(4):
            turned[big_c * 32 : big_c * 32 + 32, i * 64 : i * 64 + 64] = z5[
                i * 32 : i * 32 + 32, big_c * 64 : big_c * 64 + 64
            ]
    progress(5)
    spot = iota((128, 128), 0)
    column = over(spot, 32)
    weave = one_hot(iota((128, 128), 1) == (spot - column * 32) * 4 + column)
    parts = three_parts(turned[...])
    lined[...] = (mm_tn(parts[2], weave) + mm_tn(parts[1], weave)) + mm_tn(parts[0], weave)
    progress(6)
    for o in range(12):
        fine[o] = lined[pl.ds(o, 64, stride=16), :] + b5[0:1, o : o + 1]
    for point in range(7, 11):
        progress(point)
    drain_gather()
    for flow in flows:
        flow.drain()


def train_of(coarse, cot, weights, biases):
    count3 = count_of(3) + 16
    scratch = (
        ((28, 12, 256), BF),
        ((3, 12, 96, 128), BF),
        ((448, 256), F32),
        ((3072, 128), F32),
        ((SPAN, 128), F32),
        ((SPAN, 144), F32),
        ((144, 448), F32),
        ((SPAN, 144), BF),
        ((count_of(5) + 16, 64), F32),
        ((SPAN, 192), BF),
        ((SPAN, 192), BF),
        ((2, count3, 128), F32),
        ((2, SPAN, 256), BF),
        ((8, count3, 128), F32),
        ((4, SPAN, 384), BF),
        ((3, 1152, 128), F32),
        ((SPAN, 432), F32),
        ((288, 1152), F32),
        ((SPAN, 432), BF),
        ((512, 192), BF),
        ((8, count3, 128), F32),
        ((2, SPAN, 1024), BF),
        ((2, count_of(2) + 16, 128), F32),
        ((SPAN, 768), BF),
        ((SPAN, 192), BF),
        ((144, 64), BF),
        ((576, 256), BF),
        ((576, 256), BF),
        ((3, 256, 512), BF),
        ((4, 256, 1024), BF),
        ((3, 64, 768), BF),
        ((3, 64, 192), BF),
        ((6, 384, 256), BF),
        ((1024, 432), BF),
        ((3, 384, 512), F32),
        ((512, 256), F32),
        ((128, 1024), F32),
        ((1024, 128), F32),
        ((576, 432), F32),
        ((1536, 128), F32),
        ((1536, 128), F32),
        ((3, 384, 128), F32),
        ((384, 128), F32),
        ((3, 96, 128), F32),
        ((96, 128), F32),
        ((4, 96, 128), F32),
    )
    counts = ((2,), (16,), (16,), (16,), (12,), (3, 3), (3, 3), (8, 2), (8, 2), (8, 5, 3), (8, 5, 3))
    vmem = pl.BlockSpec(memory_space=pltpu.VMEM)
    return pl.pallas_call(
        train_kernel,
        out_shape=[
            jax.ShapeDtypeStruct((12, 64, 128), F32),
            jax.ShapeDtypeStruct((3072, 128), F32),
        ],
        in_specs=[vmem] * 12,
        out_specs=[vmem] * 2,
        scratch_shapes=[pltpu.VMEM(shape, kind) for shape, kind in scratch]
        + [pltpu.SemaphoreType.DMA(shape) for shape in counts],
        compiler_params=pltpu.CompilerParams(
            vmem_limit_bytes=66000000, collective_id=0, has_side_effects=True
        ),
        name="train_tile",
    )(coarse, cot, *weights, *biases)


def unpack_kernel(
    scale, fine_in, whole, fine, out_w1, out_w2, out_w3, out_w4, out_w5, out_b1, out_b2, out_b3, out_b4, out_b5
):
    fine[...] = fine_in[...]
    for index, target in ((0, out_w4), (1280, out_w3)):
        target[:, 0:128] = whole[index : index + 576, :] * scale
        target[:, 128:256] = whole[index + 576 : index + 1152, :] * scale
    for tap in range(9):
        lanes = slice(64 * (tap % 2), 64 * (tap % 2) + 64)
        at = 2560 + 64 * (tap // 2)
        out_w2[tap * 64 : tap * 64 + 64, :] = whole[at : at + 64, lanes] * scale
        at = 16 * (tap // 2)
        out_w1[tap] = whole[2880 + at : 2892 + at, lanes] * scale
        out_w5[tap] = whole[1152 + at : 1164 + at, lanes] * scale
    for index, target in ((1232, out_b4), (2432, out_b3)):
        target[:, 0:128] = whole[index : index + 1, :] * scale
        target[:, 128:256] = whole[index + 1 : index + 2, :] * scale
    out_b2[...] = whole[2960:2961, 0:64] * scale
    out_b1[...] = whole[2960:2961, 64:128] * scale
    out_b5[...] = whole[1234:1235, 0:12] * scale


def unpack_of(fine, whole, scale):
    shapes = ((12, 64, 128), (9, 12, 64), (576, 64), (576, 256), (576, 256), (9, 12, 64))
    shapes = shapes + ((1, 64), (1, 64), (1, 256), (1, 256), (1, 12))
    vmem = pl.BlockSpec(memory_space=pltpu.VMEM)
    return pl.pallas_call(
        functools.partial(unpack_kernel, scale),
        out_shape=[jax.ShapeDtypeStruct(shape, F32) for shape in shapes],
        in_specs=[vmem] * 2,
        out_specs=[vmem] * 11,
        name="unpack",
    )(fine, whole)


def local(
    coarse,
    weight_one,
    weight_two,
    weight_three,
    weight_four,
    weight_five,
    bias_one,
    bias_two,
    bias_three,
    bias_four,
    bias_five,
    cotangent,
):
    weights = (
        weight_one.reshape(9, 12, 64),
        weight_two.reshape(576, 64),
        weight_three.reshape(576, 256),
        weight_four.reshape(576, 256),
        weight_five.transpose(0, 1, 3, 2).reshape(9, 12, 64),
    )
    biases = tuple(
        bias.reshape(1, -1) for bias in (bias_one, bias_two, bias_three, bias_four, bias_five)
    )
    fine, whole = train_of(coarse.reshape(12, 512), cotangent, weights, biases)
    results = unpack_of(fine, whole, float(16 * 128 * 512) ** -0.5)
    return (
        results[0],
        results[1].reshape(3, 3, 12, 64),
        results[2].reshape(3, 3, 64, 64),
        results[3].reshape(3, 3, 64, 256),
        results[4].reshape(3, 3, 64, 256),
        results[5].reshape(3, 3, 12, 64).transpose(0, 1, 3, 2),
    ) + tuple(result.reshape(-1) for result in results[6:])


def solution(mesh):
    in_specs = (
        P(None, ("gx", "gy"), None),
        P(),
        P(),
        P(),
        P(),
        P(),
        P(),
        P(),
        P(),
        P(),
        P(),
        P(None, "gx", "gy"),
    )
    out_specs = (P(None, "gx", "gy"), P(), P(), P(), P(), P(), P(), P(), P(), P(), P())
    return jax.shard_map(local, mesh=mesh, in_specs=in_specs, out_specs=out_specs, check_vma=False)
```

time: 104 us -> 81.2 us (0.78)
  local copies, waits for them, and re-layouts: 13.3 us -> 0 us
  Pallas kernels: 89.2 us -> 80.3 us
    unnamed x23 -> x0, local copies, waits for them, and re-layouts: 12 us -> none
    pallas_call x3 -> x2, Pallas kernels: 89.2 us -> 80.3 us  [the longest x1 77.4 us: train_of(): pl.pallas_call(train_kernel, out_shape=[jax.ShapeDtypeStruct((12, 64, 128...]
    pad x1 -> x0, local copies, waits for them, and re-layouts: 1.33 us -> none  [local(): row = jnp.pad(coarse.reshape(12, 512), ((0, 4), (0, 0)))]
where the time goes in v1:
time: 81.2 us; the launch traced here: 81 us
  Pallas kernels  80.3 us (99%)
    pallas_call x1, Pallas kernels, train_of(): pl.pallas_call(train_kernel, out_shape=[jax.ShapeDtypeStruct((12, 64, 128...  77.4 us
    pallas_call x1, Pallas kernels, unpack_of(): pl.pallas_call(functools.partial(unpack_kernel, scale), out_shape=[jax.Sh...  2.92 us

profile of v1, /device:TPU:1, one launch (start us, length us, event | category | flops | bytes accessed | tf_op | source)
XLA Modules:
  0.0 81.0 jit_solution(11180563560380980496)
XLA Ops:
  0.6 77.4 %train_tile.1 = (f32[12,64,128]{2,1,0:T(8,128)}, f32[3072,128]{1,0:T(8,128)}) custom-call(bf16[12,512]{1,0:T(8,128)(2,1)} %bitcast.30, bf16[12,64,128]{2,1,0:T(8,128)(2,1)} %cot.1, bf16[9,12,64]{2,1,0:T(8,128)(2,1)} %bitcast.28, bf16[576,64]{1,0:T(8,128)(2,1)} %bitcast.27, bf16[576,256]{1,0:T(8,128)(2,1)} %bitcast.25, bf16[576,256]{1,0:T(8,128)(2,1)} %bitcast.26, ...), custom_call_target="tpu_custom_call" | custom-call | tf_op jit(solution)/shard_map/train_tile/pallas_call | solution.py:922
  78.1 2.9 %unpack.1 = (f32[12,64,128]{2,1,0:T(8,128)}, f32[9,12,64]{2,1,0:T(8,128)}, f32[576,64]{1,0:T(8,128)}, f32[576,256]{1,0:T(8,128)}, f32[576,256]{1,0:T(8,128)}, /*...) custom-call(f32[12,64,128]{2,1,0:T(8,128)} %get-tuple-element.24.fin, ...), custom_call_target="tpu_custom_call" | custom-call | tf_op jit(solution)/shard_map/unpack/pallas_call | solution.py:965

commit v2 on v1

--- a/solution.py
+++ b/solution.py
@@ -28,37 +28,53 @@
 
 
 def rows_at(start, count):
-    return pl.ds(pl.multiple_of(start, 8), count)
-
-
+    return pl.ds(pl.multiple_of(start, 16), count)
+
+
+PACK = 2816
 FLOWS = (
-    (0, 512, (0, 1, 2)),
-    (512, 512, (1, 2, 0)),
-    (1024, 256, (2, 0, 1)),
-    (1280, 512, (1, 2, 0)),
-    (1792, 512, (2, 0, 1)),
-    (2304, 256, (0, 1, 2)),
-    (2560, 256, (0, 1, 2)),
-    (2816, 256, (1, 2, 0)),
+    (0, 512, (0, 1, 2), False),
+    (512, 512, (1, 2, 0), False),
+    (1024, 128, (2, 0, 1), True),
+    (1152, 512, (1, 2, 0), False),
+    (1664, 512, (2, 0, 1), False),
+    (2176, 128, (0, 1, 2), True),
+    (2304, 256, (0, 1, 2), True),
+    (2560, 128, (1, 2, 0), True),
+    (2688, 128, (2, 0, 1), True),
 )
-WHEN_READY = (0, 0, 0, 2, 2, 2, 3, 3)
+LAYER_FOUR, LAYER_THREE, OTHERS = (0, 1, 2), (3, 4, 5), (6, 7, 8)
+
+
+def first_place(tap):
+    if tap < 5:
+        return 2560 + 12 * tap, slice(64, 128)
+    at = 2624 + 16 * ((tap - 5) // 2)
+    return at, slice(64 * ((tap - 5) % 2), 64 * ((tap - 5) % 2) + 64)
+
+
+def last_place(tap):
+    return 2656 + 12 * (tap // 2), slice(64 * (tap % 2), 64 * (tap % 2) + 64)
 
 
 class Flow:
-    def __init__(self, number, place, core, pack, whole, base, rows, order):
+    def __init__(self, number, place, core, pack, whole, base, rows, order, short):
         self.number, self.place, self.core = number, place, core
         self.pack, self.whole = pack, whole
         self.base, self.order = base, order
-        self.sizes = (rows // 2, rows // 8, rows // 32)
+        self.eighth, self.short = rows // 8, short
+        before = [flow for flow in FLOWS[:number] if flow[3] == short]
+        self.late_at = sum(flow[1] for flow in before) // (8 if short else 32)
+        self.hop = 0
         self.sent = []
         self.now = []
 
-    def send(self, src, dst, sem, index, peer):
+    def send(self, src, dst, slot, peer):
         copy = pltpu.make_async_remote_copy(
             src_ref=src,
             dst_ref=dst,
-            send_sem=self.sems[sem].at[index],
-            recv_sem=self.sems[sem + 1].at[index],
+            send_sem=self.sems[0].at[self.number, self.hop + slot],
+            recv_sem=self.sems[1].at[self.number, self.hop + slot],
             device_id=peer,
             device_id_type=MESH_ID,
         )
@@ -71,90 +87,109 @@
             copy.wait_recv()
         self.now = []
 
-    def to_partner(self, src, dst, index):
-        self.send(src, dst, 0, (self.number, index), device_at(self.place, 1 - self.core))
-
-    def to_axis(self, turn, hop, views):
+    def to_eight(self, views):
+        axis = self.order[0]
+        for other in range(2):
+            for step in range(4):
+                slot = other * 4 + step
+                if slot > 0:
+                    core = (self.core + other) % 2
+                    spot = along(self.place, axis, step)
+                    src, dst = views(slot, spot[axis] * 2 + core)
+                    self.send(src, dst, slot, device_at(spot, core))
+        self.hop += 8
+
+    def to_axis(self, turn, views):
         axis = self.order[turn]
         for step in (1, 2, 3):
             src, dst = views(axis, step)
-            self.send(
-                src,
-                dst,
-                2,
-                (self.number, hop, step - 1),
-                device_at(along(self.place, axis, step), self.core),
-            )
-
-    def row(self, level):
-        row = self.base + self.core * self.sizes[0]
-        for turn in range(level):
-            row = row + self.place[self.order[turn]] * self.sizes[turn + 1]
-        return row
+            self.send(src, dst, step, device_at(along(self.place, axis, step), self.core))
+        self.hop += 4
 
     def advance(self, stage):
-        pair_in, pair_sum, in_a, sum_a, in_b, sum_b, in_c = self.refs
-        half, fourth, small = self.sizes
-        two, eight, many = self.base // 2, self.base // 8, self.base // 32
+        in_a, sum_a, in_b, in_c, in_d = self.refs
+        eighth, small = self.eighth, self.eighth // 4
+        mine = self.place[self.order[0]] * 2 + self.core
+        eight, many = self.base // 8, self.late_at
+        row = self.base + mine * eighth
         if stage == 0:
-            self.to_partner(
-                self.pack.at[rows_at(self.base + (1 - self.core) * half, half)],
-                pair_in.at[pl.ds(two, half)],
-                0,
+            self.to_eight(
+                lambda slot, chunk: (
+                    self.pack.at[rows_at(self.base + chunk * eighth, eighth)],
+                    in_a.at[slot, pl.ds(eight, eighth)],
+                )
             )
             return
         self.arrive()
         if stage == 1:
-            own = self.pack[rows_at(self.base + self.core * half, half), :]
-            pair_sum[pl.ds(two, half), :] = own + pair_in[pl.ds(two, half), :]
-            self.to_axis(
-                0,
-                0,
-                lambda axis, step: (
-                    pair_sum.at[rows_at(two + (self.place[axis] + step) % 4 * fourth, fourth)],
-                    in_a.at[step - 1, pl.ds(eight, fourth)],
-                ),
-            )
-        elif stage == 2:
-            value = pair_sum[rows_at(two + self.place[self.order[0]] * fourth, fourth), :]
-            for step in range(3):
-                value = value + in_a[step, pl.ds(eight, fourth), :]
-            sum_a[pl.ds(eight, fourth), :] = value
-            self.to_axis(
-                1,
-                1,
-                lambda axis, step: (
-                    sum_a.at[rows_at(eight + (self.place[axis] + step) % 4 * small, small)],
-                    in_b.at[step - 1, pl.ds(many, small)],
-                ),
-            )
-        elif stage == 3:
+            value = self.pack[rows_at(row, eighth), :]
+            for slot in range(1, 8):
+                value = value + in_a[slot, pl.ds(eight, eighth), :]
+            if self.short:
+                at = self.late_at
+                in_d[0, pl.ds(at, eighth), :] = value
+                for step_b in range(4):
+                    for step_c in range(4):
+                        slot = step_b * 4 + step_c
+                        if slot > 0:
+                            spot = along(self.place, self.order[1], step_b)
+                            spot = along(spot, self.order[2], step_c)
+                            self.send(
+                                in_d.at[0, pl.ds(at, eighth)],
+                                in_d.at[slot, pl.ds(at, eighth)],
+                                slot,
+                                device_at(spot, self.core),
+                            )
+                self.hop += 16
+            else:
+                sum_a[pl.ds(eight, eighth), :] = value
+                self.to_axis(
+                    1,
+                    lambda axis, step: (
+                        sum_a.at[rows_at(eight + (self.place[axis] + step) % 4 * small, small)],
+                        in_b.at[step - 1, pl.ds(many, small)],
+                    ),
+                )
+            return
+        if self.short:
+            if stage == 2:
+                at = self.late_at
+                total = None
+                for spot_b in range(4):
+                    for spot_c in range(4):
+                        slot = (self.place[self.order[1]] - spot_b + 4) % 4 * 4
+                        slot = slot + (self.place[self.order[2]] - spot_c + 4) % 4
+                        term = in_d[slot, pl.ds(at, eighth), :]
+                        total = term if total is None else total + term
+                self.whole[rows_at(row, eighth), :] = total.astype(jnp.bfloat16)
+                self.spread(row)
+            return
+        if stage == 2:
             value = sum_a[rows_at(eight + self.place[self.order[1]] * small, small), :]
             for step in range(3):
                 value = value + in_b[step, pl.ds(many, small), :]
             in_c[0, pl.ds(many, small), :] = value
             self.to_axis(
                 2,
-                2,
                 lambda axis, step: (
                     in_c.at[0, pl.ds(many, small)],
                     in_c.at[step, pl.ds(many, small)],
                 ),
             )
-        elif stage == 4:
+        elif stage == 3:
             here = self.place[self.order[2]]
             terms = [in_c[(here - other + 4) % 4, pl.ds(many, small), :] for other in range(4)]
-            self.whole[rows_at(self.row(2), small), :] = (terms[0] + terms[1]) + (
-                terms[2] + terms[3]
-            )
-            block = self.whole.at[rows_at(self.row(2), small)]
-            self.to_axis(1, 3, lambda axis, step: (block, block))
-        elif stage == 5:
-            block = self.whole.at[rows_at(self.row(1), fourth)]
-            self.to_axis(0, 4, lambda axis, step: (block, block))
-        elif stage == 6:
-            block = self.whole.at[rows_at(self.row(0), half)]
-            self.to_partner(block, block, 1)
+            at = row + self.place[self.order[1]] * small
+            total = (terms[0] + terms[1]) + (terms[2] + terms[3])
+            self.whole[rows_at(at, small), :] = total.astype(jnp.bfloat16)
+            block = self.whole.at[rows_at(at, small)]
+            self.to_axis(1, lambda axis, step: (block, block))
+        elif stage == 4:
+            self.spread(row)
+
+    def spread(self, row):
+        block = self.whole.at[rows_at(row, self.eighth)]
+        self.to_eight(lambda slot, chunk: (block, block))
 
     def drain(self):
         for copy in self.sent:
@@ -297,13 +332,11 @@
     turned,
     lined,
     wide,
-    pair_in,
-    pair_sum,
     in_a,
     sum_a,
     in_b,
-    sum_b,
     in_c,
+    in_d,
     keep_sem,
     row_send,
     row_recv,
@@ -311,8 +344,6 @@
     far_recv,
     cot_send,
     cot_recv,
-    pair_send,
-    pair_recv,
     hop_send,
     hop_recv,
 ):
@@ -331,14 +362,15 @@
                 )
     spot_now, core = coordinates()
     partner = device_at(spot_now, 1 - core)
+    helpers = [partner]
     for axis in range(3):
         for step in (1, 2, 3):
-            pl.semaphore_signal(
-                barrier,
-                inc=1,
-                device_id=device_at(along(spot_now, axis, step), core),
-                device_id_type=MESH_ID,
-            )
+            near = along(spot_now, axis, step)
+            helpers += [device_at(near, core), device_at(near, 1 - core)]
+            for more in (1, 2, 3):
+                helpers.append(device_at(along(near, (axis + 1) % 3, more), core))
+    for helper in helpers:
+        pl.semaphore_signal(barrier, inc=1, device_id=helper, device_id_type=MESH_ID)
     locals_ = [
         pltpu.make_async_copy(
             cot, cot_in.at[1, :, pl.ds(16, 64), :], keep_sem.at[0]
@@ -349,7 +381,7 @@
     ]
     for copy in locals_:
         copy.start()
-    pl.semaphore_wait(barrier, 56)
+    pl.semaphore_wait(barrier, 47 + len(helpers))
 
     def remote(src, dst, send_sem, recv_sem, target):
         return pltpu.make_async_remote_copy(
@@ -371,14 +403,14 @@
             target,
         )
 
-    copies = []
+    cot_copies = []
     parts = ((16, 48, 0), (64, 0, 16), (16, 0, 80))
     for index_x, step_x in enumerate((1, 0, -1)):
         count, src_row, dst_row = parts[index_x]
         for index_y, step_y in enumerate((1, 0, -1)):
             if step_x == 0 and step_y == 0:
                 continue
-            copies.append(
+            cot_copies.append(
                 remote(
                     cot.at[:, pl.ds(src_row, count), :],
                     cot_in.at[index_y, :, pl.ds(dst_row, count), :],
@@ -387,6 +419,10 @@
                     peer(step_x, step_y),
                 )
             )
+    for copy in cot_copies:
+        copy.start()
+
+    copies = []
     for step in range(1, 16):
         copies.append(row_copy(step, 6 + gy, row_send.at[step], row_recv.at[step], 0))
     for copy in copies:
@@ -420,11 +456,11 @@
 
     def await_cot():
         locals_[0].wait()
-        for copy in copies[:8]:
+        for copy in cot_copies:
             copy.wait_recv()
 
     def drain_gather():
-        for copy in copies:
+        for copy in copies + cot_copies:
             copy.wait_send()
 
         @pl.when(gy < 6)
@@ -442,17 +478,15 @@
         Flow(number, spot_now, core, pack, whole, *FLOWS[number])
         for number in range(len(FLOWS))
     ]
-    refs = (pair_in, pair_sum, in_a, sum_a, in_b, sum_b, in_c)
-    sems = (pair_send, pair_recv, hop_send, hop_recv)
+    refs = (in_a, sum_a, in_b, in_c, in_d)
+    sems = (hop_send, hop_recv)
     for flow in flows:
         flow.refs = refs
         flow.sems = sems
 
-    def progress(point):
-        for number, flow in enumerate(flows):
-            stage = point - WHEN_READY[number]
-            if 0 <= stage < 8:
-                flow.advance(stage)
+    def progress(numbers, stage):
+        for number in numbers:
+            flows[number].advance(stage)
 
     base_row = gx * 16
     base_col = gy * 32
@@ -564,91 +598,8 @@
     t_c1[...] = jnp.zeros(t_c1.shape, F32)
     t_cot[...] = jnp.zeros(t_cot.shape, F32)
     known[...] = jnp.zeros(known.shape, F32)
-    for first, last in ((1152, 1280), (2432, 2560), (2816, 3072)):
+    for first, last in ((2560, 2816),):
         pack[first:last, :] = jnp.zeros((last - first, 128), F32)
-
-    spot = iota((144, 256), 0)
-    tap_col = over(spot, 48)
-    want = spot - tap_col * 48 - 8 + tap_col - 1 + base_col
-    first = jnp.clip(jnp.right_shift(base_col - 8, 7), 0, 2) * 128
-    pick = one_hot((want == iota((144, 256), 1) + first) & (want >= 0) & (want < 512))
-    await_rows()
-    for k in range(28):
-        present = (base_row - 6 + k >= 0) & (base_row - 6 + k < 128)
-        known[k * 16 : k * 16 + 12, :] = jnp.where(present, rows_in[k].astype(F32), 0.0)
-    m_c1[...] = mm_nt(pick, known[...].astype(BF))
-    for i in range(-5, 21):
-        for s in range(3):
-            at = (i + 7) * STRIDE - 8
-            t_c1[at : at + 48, s * 48 : s * 48 + 48] = m_c1[
-                s * 48 : s * 48 + 48, (i + 5) * 16 : (i + 5) * 16 + 48
-            ]
-    x1[...] = t_c1[...].astype(BF)
-
-    def three_shifts(target, begin, count):
-        t64[8 + count : 16 + count, :] = jnp.zeros((8, 64), F32)
-        for s in range(3):
-            target[begin : begin + count, s * 64 : s * 64 + 64] = t64[7 + s : 7 + s + count, :].astype(BF)
-
-    begin, count = start_of(5), count_of(5)
-
-    def one(at):
-        z = mm(x1[slab(begin + at, 256), :], v1[...]) + b1[...]
-        t64[pl.ds(pl.multiple_of(8 + at, 8), 256), :] = (
-            jnp.tanh(z) * kept(begin + at, 256)
-        )
-
-    blocks(count, 256, one)
-    three_shifts(x2, begin, count)
-
-    begin2, count2 = start_of(4), count_of(4)
-
-    def two(at):
-        z = b2[...]
-        for r in range(3):
-            z = z + mm(x2[slab(begin2 + 48 * (r - 1) + at, 592), :], w2[192 * r : 192 * r + 192, :])
-        t64[pl.ds(pl.multiple_of(8 + at, 8), 592), :] = jnp.tanh(z) * kept(begin2 + at, 592)
-
-    blocks(count2, 592, two)
-    three_shifts(x3, begin2, count2)
-
-    begin3, count3 = start_of(3), count_of(3)
-
-    def three(at):
-        z = bias3
-        for r in range(3):
-            z = z + mm(x3[slab(begin3 + 48 * (r - 1) + at, 272), :], v3[192 * r : 192 * r + 192, :])
-        z = jnp.tanh(z) * kept(begin3 + at, 272)
-        for a in range(2):
-            t3[a, pl.ds(pl.multiple_of(8 + at, 8), 272), :] = z[:, a * 128 : a * 128 + 128]
-
-    blocks(count3, 272, three)
-    for a in range(2):
-        at = slice(begin3, begin3 + count3)
-        x4[a, at, 0:128] = t3[a, 8 : 8 + count3, :].astype(BF)
-        x4[a, at, 128:192] = t3[a, 9 : 9 + count3, 0:64].astype(BF)
-        x4[a, at, 192:256] = t3[a, 7 : 7 + count3, 64:128].astype(BF)
-
-    def four(at):
-        for p in range(2):
-            z = jnp.concatenate([bias4, bias4], axis=1)
-            for r in range(3):
-                a, d = ROW_SOURCE[p][r]
-                z = z + mm(x4[a, slab(begin3 + 48 * d + at, 272), :], v4f[r])
-            z = jnp.tanh(z) * kept(begin3 + at, 272)
-            for half in range(2):
-                for q in range(2):
-                    t4[4 * p + 2 * half + q, pl.ds(pl.multiple_of(8 + at, 8), 272), :] = z[
-                        :, q * 256 + half * 128 : q * 256 + half * 128 + 128
-                    ]
-
-    blocks(count3, 272, four)
-    for big_r in range(4):
-        at = slice(begin3, begin3 + count3)
-        x5[big_r, at, 0:128] = t4[2 * big_r, 8 : 8 + count3, :].astype(BF)
-        x5[big_r, at, 128:256] = t4[2 * big_r + 1, 8 : 8 + count3, :].astype(BF)
-        x5[big_r, at, 256:320] = t4[2 * big_r, 9 : 9 + count3, 0:64].astype(BF)
-        x5[big_r, at, 320:384] = t4[2 * big_r + 1, 7 : 7 + count3, 64:128].astype(BF)
 
     await_cot()
     fine_row = iota((96, 128), 0) - 16 + gx * 64
@@ -678,6 +629,176 @@
         at = (big_c + 1) * 72 + 12
         g5[:, big_c * 48 : big_c * 48 + 48] = inner(t_cot, 0, slice(at, at + 48)).astype(BF)
 
+    spot = iota((144, 256), 0)
+    tap_col = over(spot, 48)
+    want = spot - tap_col * 48 - 8 + tap_col - 1 + base_col
+    first = jnp.clip(jnp.right_shift(base_col - 8, 7), 0, 2) * 128
+    pick = one_hot((want == iota((144, 256), 1) + first) & (want >= 0) & (want < 512))
+    await_rows()
+    for k in range(28):
+        present = (base_row - 6 + k >= 0) & (base_row - 6 + k < 128)
+        known[k * 16 : k * 16 + 12, :] = jnp.where(present, rows_in[k].astype(F32), 0.0)
+    m_c1[...] = mm_nt(pick, known[...].astype(BF))
+    for i in range(-5, 21):
+        for s in range(3):
+            at = (i + 7) * STRIDE - 8
+            t_c1[at : at + 48, s * 48 : s * 48 + 48] = m_c1[
+                s * 48 : s * 48 + 48, (i + 5) * 16 : (i + 5) * 16 + 48
+            ]
+    x1[...] = t_c1[...].astype(BF)
+
+    def three_shifts(target, begin, count):
+        t64[8 + count : 16 + count, :] = jnp.zeros((8, 64), F32)
+        for s in range(3):
+            target[begin : begin + count, s * 64 : s * 64 + 64] = t64[7 + s : 7 + s + count, :].astype(BF)
+
+    begin, count = start_of(5), count_of(5)
+
+    def one(at):
+        z = mm(x1[slab(begin + at, 256), :], v1[...]) + b1[...]
+        t64[pl.ds(pl.multiple_of(8 + at, 8), 256), :] = (
+            jnp.tanh(z) * kept(begin + at, 256)
+        )
+
+    blocks(count, 256, one)
+    three_shifts(x2, begin, count)
+
+    begin2, count2 = start_of(4), count_of(4)
+
+    def two(at):
+        z = b2[...]
+        for r in range(3):
+            z = z + mm(x2[slab(begin2 + 48 * (r - 1) + at, 592), :], w2[192 * r : 192 * r + 192, :])
+        t64[pl.ds(pl.multiple_of(8 + at, 8), 592), :] = jnp.tanh(z) * kept(begin2 + at, 592)
+
+    blocks(count2, 592, two)
+    three_shifts(x3, begin2, count2)
+
+    begin3, count3 = start_of(3), count_of(3)
+
+    def three(at):
+        z = bias3
+        for r in range(3):
+            z = z + mm(x3[slab(begin3 + 48 * (r - 1) + at, 272), :], v3[192 * r : 192 * r + 192, :])
+        z = jnp.tanh(z) * kept(begin3 + at, 272)
+        for a in range(2):
+            t3[a, pl.ds(pl.multiple_of(8 + at, 8), 272), :] = z[:, a * 128 : a * 128 + 128]
+
+    blocks(count3, 272, three)
+    for a in range(2):
+        at = slice(begin3, begin3 + count3)
+        x4[a, at, 0:128] = t3[a, 8 : 8 + count3, :].astype(BF)
+        x4[a, at, 128:192] = t3[a, 9 : 9 + count3, 0:64].astype(BF)
+        x4[a, at, 192:256] = t3[a, 7 : 7 + count3, 64:128].astype(BF)
+
+    def four(at):
+        for p in range(2):
+            z = jnp.concatenate([bias4, bias4], axis=1)
+            for r in range(3):
+                a, d = ROW_SOURCE[p][r]
+                z = z + mm(x4[a, slab(begin3 + 48 * d + at, 272), :], v4f[r])
+            z = jnp.tanh(z) * kept(begin3 + at, 272)
+            for half in range(2):
+                for q in range(2):
+                    t4[4 * p + 2 * half + q, pl.ds(pl.multiple_of(8 + at, 8), 272), :] = z[
+                        :, q * 256 + half * 128 : q * 256 + half * 128 + 128
+                    ]
+
+    blocks(count3, 272, four)
+    for big_r in range(4):
+        at = slice(begin3, begin3 + count3)
+        x5[big_r, at, 0:128] = t4[2 * big_r, 8 : 8 + count3, :].astype(BF)
+        x5[big_r, at, 128:256] = t4[2 * big_r + 1, 8 : 8 + count3, :].astype(BF)
+        x5[big_r, at, 256:320] = t4[2 * big_r, 9 : 9 + count3, 0:64].astype(BF)
+        x5[big_r, at, 320:384] = t4[2 * big_r + 1, 7 : 7 + count3, 64:128].astype(BF)
+
+    def back_four(at):
+        here = slab(begin3 + at, 272)
+        keep = kept(begin3 + at, 272)
+        for big_r in range(4):
+            value = mm_nt(xc[here, :], v5b[big_r * 256 : big_r * 256 + 256, :])
+            act = x5[big_r, here, 0:256].astype(F32)
+            value = value * (1.0 - act * act) * keep
+            for q in range(2):
+                t_g4[2 * big_r + q, pl.ds(pl.multiple_of(8 + at, 8), 272), :] = value[
+                    :, q * 128 : q * 128 + 128
+                ]
+
+    blocks(count3, 272, back_four)
+    for p in range(2):
+        at = slice(begin3, begin3 + count3)
+        for half in range(2):
+            src = (2 * p + half) * 2
+            dst = half * 128
+            for q in range(2):
+                g4[p, at, q * 256 + dst : q * 256 + dst + 128] = t_g4[
+                    src + q, 8 : 8 + count3, :
+                ].astype(BF)
+            g4[p, at, 512 + dst : 640 + dst] = t_g4[src, 9 : 9 + count3, :].astype(BF)
+            g4[p, at, 768 + dst : 896 + dst] = t_g4[src + 1, 7 : 7 + count3, :].astype(BF)
+
+    sums4 = jnp.zeros((1, 256), F32)
+    for p in range(2):
+        value = inner(g4.at[p], 0, slice(0, 512))
+        sums = jnp.sum(value.astype(F32), axis=0, keepdims=True)
+        sums4 = sums4 + sums[:, 0:256] + sums[:, 256:512]
+        for r in range(3):
+            a, d = ROW_SOURCE[p][r]
+            term = mm_tn(inner(x4.at[a], d, slice(0, 256)), value)
+            if p == 0:
+                acc[r, 0:256, :] = term
+            else:
+                acc[r, 0:256, :] = acc[r, 0:256, :] + term
+    for r in range(3):
+        for s in range(3):
+            one_at = PAIR_ORDER.index(s) * 64
+            two_at = PAIR_ORDER.index(s + 1) * 64
+            value = acc[r, one_at : one_at + 64, 0:256] + acc[r, two_at : two_at + 64, 256:512]
+            value = exact_right(value, to_natural)
+            at = (r * 3 + s) * 64
+            pack[at : at + 64, :] = value[:, 0:128]
+            pack[576 + at : 640 + at, :] = value[:, 128:256]
+    sums4 = exact_right(jnp.broadcast_to(sums4, (8, 256)), to_natural)
+    pack[2720:2721, :] = sums4[0:1, 0:128]
+    pack[2721:2722, :] = sums4[0:1, 128:256]
+
+    progress(LAYER_FOUR, 0)
+
+    begin2, count2 = start_of(2), count_of(2)
+
+    def back_three(at):
+        value = None
+        for u in range(4):
+            p, d = BACK_SOURCE[u]
+            term = mm_nt(g4[p, slab(begin2 + 48 * d + at, 496), :], v4b[u])
+            value = term if value is None else value + term
+        here = slab(begin2 + at, 496)
+        act = jnp.concatenate([x4[0, here, 0:128], x4[1, here, 0:128]], axis=1).astype(F32)
+        value = value * (1.0 - act * act) * kept(begin2 + at, 496)
+        for a in range(2):
+            t_g3[a, pl.ds(pl.multiple_of(8 + at, 8), 496), :] = value[:, a * 128 : a * 128 + 128]
+
+    blocks(count2, 496, back_three)
+    for v in range(3):
+        for a in range(2):
+            at = v * 256 + a * 128
+            g3[begin2 : begin2 + count2, at : at + 128] = t_g3[a, 7 + v : 7 + v + count2, :].astype(BF)
+
+    value = inner(g3, 0, slice(256, 512))
+    sums3 = jnp.sum(value.astype(F32), axis=0, keepdims=True)
+    for r in range(3):
+        term = mm_tn(inner(x3, r - 1, slice(0, 192)), value)
+        term = exact_right(term, to_natural)
+        at = 1152 + r * 192
+        pack[at : at + 192, :] = term[:, 0:128]
+        pack[576 + at : 768 + at, :] = term[:, 128:256]
+    sums3 = exact_right(jnp.broadcast_to(sums3, (8, 256)), to_natural)
+    pack[2722:2723, :] = sums3[0:1, 0:128]
+    pack[2723:2724, :] = sums3[0:1, 128:256]
+
+    progress(LAYER_THREE, 0)
+    progress(LAYER_FOUR, 1)
+
     lanes5 = iota((384, 192), 1)
     cell5 = over(lanes5, 12)
     col5 = over(cell5, 4)
@@ -703,100 +824,12 @@
             tap = r * 3 + s
             parts = three_parts(value)
             value = (mm_nt(fold, parts[2]) + mm_nt(fold, parts[1])) + mm_nt(fold, parts[0])
-            at = 1152 + 16 * (tap // 2)
-            pack[at : at + 16, 64 * (tap % 2) : 64 * (tap % 2) + 64] = value
+            at, lanes = last_place(tap)
+            pack[at : at + 12, lanes] = value[0:12]
     sums5 = jnp.sum(g5[...].astype(F32), axis=0, keepdims=True)
     fold_lane = iota((192, 128), 0)
     fold = one_hot((fold_lane - over(fold_lane, 12) * 12) == iota((192, 128), 1))
-    pack[1234:1235, :] = exact_right(jnp.broadcast_to(sums5, (8, 192)), fold)[0:1]
-
-    def back_four(at):
-        here = slab(begin3 + at, 272)
-        keep = kept(begin3 + at, 272)
-        for big_r in range(4):
-            value = mm_nt(xc[here, :], v5b[big_r * 256 : big_r * 256 + 256, :])
-            act = x5[big_r, here, 0:256].astype(F32)
-            value = value * (1.0 - act * act) * keep
-            for q in range(2):
-                t_g4[2 * big_r + q, pl.ds(pl.multiple_of(8 + at, 8), 272), :] = value[
-                    :, q * 128 : q * 128 + 128
-                ]
-
-    blocks(count3, 272, back_four)
-    for p in range(2):
-        at = slice(begin3, begin3 + count3)
-        for half in range(2):
-            src = (2 * p + half) * 2
-            dst = half * 128
-            for q in range(2):
-                g4[p, at, q * 256 + dst : q * 256 + dst + 128] = t_g4[
-                    src + q, 8 : 8 + count3, :
-                ].astype(BF)
-            g4[p, at, 512 + dst : 640 + dst] = t_g4[src, 9 : 9 + count3, :].astype(BF)
-            g4[p, at, 768 + dst : 896 + dst] = t_g4[src + 1, 7 : 7 + count3, :].astype(BF)
-
-    sums4 = jnp.zeros((1, 256), F32)
-    for p in range(2):
-        value = inner(g4.at[p], 0, slice(0, 512))
-        sums = jnp.sum(value.astype(F32), axis=0, keepdims=True)
-        sums4 = sums4 + sums[:, 0:256] + sums[:, 256:512]
-        for r in range(3):
-            a, d = ROW_SOURCE[p][r]
-            term = mm_tn(inner(x4.at[a], d, slice(0, 256)), value)
-            if p == 0:
-                acc[r, 0:256, :] = term
-            else:
-                acc[r, 0:256, :] = acc[r, 0:256, :] + term
-    for r in range(3):
-        for s in range(3):
-            one_at = PAIR_ORDER.index(s) * 64
-            two_at = PAIR_ORDER.index(s + 1) * 64
-            value = acc[r, one_at : one_at + 64, 0:256] + acc[r, two_at : two_at + 64, 256:512]
-            value = exact_right(value, to_natural)
-            at = (r * 3 + s) * 64
-            pack[at : at + 64, :] = value[:, 0:128]
-            pack[576 + at : 640 + at, :] = value[:, 128:256]
-    sums4 = exact_right(jnp.broadcast_to(sums4, (8, 256)), to_natural)
-    pack[1232:1233, :] = sums4[0:1, 0:128]
-    pack[1233:1234, :] = sums4[0:1, 128:256]
-
-    progress(0)
-
-    begin2, count2 = start_of(2), count_of(2)
-
-    def back_three(at):
-        value = None
-        for u in range(4):
-            p, d = BACK_SOURCE[u]
-            term = mm_nt(g4[p, slab(begin2 + 48 * d + at, 496), :], v4b[u])
-            value = term if value is None else value + term
-        here = slab(begin2 + at, 496)
-        act = jnp.concatenate([x4[0, here, 0:128], x4[1, here, 0:128]], axis=1).astype(F32)
-        value = value * (1.0 - act * act) * kept(begin2 + at, 496)
-        for a in range(2):
-            t_g3[a, pl.ds(pl.multiple_of(8 + at, 8), 496), :] = value[:, a * 128 : a * 128 + 128]
-
-    blocks(count2, 496, back_three)
-    for v in range(3):
-        for a in range(2):
-            at = v * 256 + a * 128
-            g3[begin2 : begin2 + count2, at : at + 128] = t_g3[a, 7 + v : 7 + v + count2, :].astype(BF)
-
-    progress(1)
-
-    value = inner(g3, 0, slice(256, 512))
-    sums3 = jnp.sum(value.astype(F32), axis=0, keepdims=True)
-    for r in range(3):
-        term = mm_tn(inner(x3, r - 1, slice(0, 192)), value)
-        term = exact_right(term, to_natural)
-        at = 1280 + r * 192
-        pack[at : at + 192, :] = term[:, 0:128]
-        pack[576 + at : 768 + at, :] = term[:, 128:256]
-    sums3 = exact_right(jnp.broadcast_to(sums3, (8, 256)), to_natural)
-    pack[2432:2433, :] = sums3[0:1, 0:128]
-    pack[2433:2434, :] = sums3[0:1, 128:256]
-
-    progress(2)
+    pack[2725:2726, :] = exact_right(jnp.broadcast_to(sums5, (8, 192)), fold)[0:1]
 
     begin1, count1 = start_of(1), count_of(1)
 
@@ -813,13 +846,16 @@
     blocks(count1, 448, back_two)
     three_shifts(g2, begin1, count1)
 
+    progress(LAYER_FOUR, 2)
+    progress(LAYER_THREE, 1)
+
     value = inner(g2, 0, slice(64, 128))
     sums2 = jnp.sum(value.astype(F32), axis=0, keepdims=True)
     for r in range(3):
         term = mm_tn(inner(x2, r - 1, slice(0, 192)), value)
         for s in range(3):
             tap = r * 3 + s
-            at = 2560 + 64 * (tap // 2)
+            at = 2304 + 64 * (tap // 2)
             pack[at : at + 64, 64 * (tap % 2) : 64 * (tap % 2) + 64] = term[s * 64 : s * 64 + 64, :]
     value = None
     for u in range(3):
@@ -828,40 +864,43 @@
     act = inner(x2, 0, slice(64, 128)).astype(F32)
     value = (value * (1.0 - act * act)).astype(BF)
     sums1 = jnp.sum(value.astype(F32), axis=0, keepdims=True)
-    pack[2960:2961, 0:64] = sums2
-    pack[2960:2961, 64:128] = sums1
+    pack[2724:2725, 0:64] = sums2
+    pack[2724:2725, 64:128] = sums1
     term = mm_tn(inner(x1, 0, slice(0, 144)), value)
     for r in range(3):
         for s in range(3):
             tap = r * 3 + s
-            at = 2880 + 16 * (tap // 2)
-            pack[at : at + 16, 64 * (tap % 2) : 64 * (tap % 2) + 64] = term[
-                s * 48 + r * 16 : s * 48 + r * 16 + 16, :
-            ]
-    progress(3)
+            at, lanes = first_place(tap)
+            pack[at : at + 12, lanes] = term[s * 48 + r * 16 : s * 48 + r * 16 + 12, :]
+    progress(OTHERS, 0)
 
     z = jnp.zeros((512, 256), F32)
     for t in range(6):
         big_r, d = FINE_SOURCE[t]
         z = z + mm(inner(x5.at[big_r], d, slice(0, 384)), v5f[t])
     z5[...] = z
-    progress(4)
+    progress(LAYER_FOUR, 3)
+    progress(LAYER_THREE, 2)
     for i in range(16):
         for big_c in range(4):
             turned[big_c * 32 : big_c * 32 + 32, i * 64 : i * 64 + 64] = z5[
                 i * 32 : i * 32 + 32, big_c * 64 : big_c * 64 + 64
             ]
-    progress(5)
+    progress(OTHERS, 1)
     spot = iota((128, 128), 0)
     column = over(spot, 32)
     weave = one_hot(iota((128, 128), 1) == (spot - column * 32) * 4 + column)
     parts = three_parts(turned[...])
     lined[...] = (mm_tn(parts[2], weave) + mm_tn(parts[1], weave)) + mm_tn(parts[0], weave)
-    progress(6)
+    progress(LAYER_FOUR, 4)
+    progress(LAYER_THREE, 3)
     for o in range(12):
         fine[o] = lined[pl.ds(o, 64, stride=16), :] + b5[0:1, o : o + 1]
-    for point in range(7, 11):
-        progress(point)
+    progress(OTHERS, 2)
+    progress(LAYER_FOUR, 5)
+    progress(LAYER_THREE, 4)
+    progress(OTHERS, 3)
+    progress(LAYER_THREE, 5)
     drain_gather()
     for flow in flows:
         flow.drain()
@@ -873,7 +912,7 @@
         ((28, 12, 256), BF),
         ((3, 12, 96, 128), BF),
         ((448, 256), F32),
-        ((3072, 128), F32),
+        ((PACK, 128), F32),
         ((SPAN, 128), F32),
         ((SPAN, 144), F32),
         ((144, 448), F32),
@@ -909,21 +948,19 @@
         ((128, 1024), F32),
         ((1024, 128), F32),
         ((576, 432), F32),
-        ((1536, 128), F32),
-        ((1536, 128), F32),
-        ((3, 384, 128), F32),
-        ((384, 128), F32),
-        ((3, 96, 128), F32),
-        ((96, 128), F32),
-        ((4, 96, 128), F32),
+        ((8, PACK // 8, 128), F32),
+        ((PACK // 8, 128), F32),
+        ((3, 64, 128), F32),
+        ((4, 64, 128), F32),
+        ((16, 96, 128), F32),
     )
-    counts = ((2,), (16,), (16,), (16,), (12,), (3, 3), (3, 3), (8, 2), (8, 2), (8, 5, 3), (8, 5, 3))
+    counts = ((2,), (16,), (16,), (16,), (12,), (3, 3), (3, 3), (9, 32), (9, 32))
     vmem = pl.BlockSpec(memory_space=pltpu.VMEM)
     return pl.pallas_call(
         train_kernel,
         out_shape=[
             jax.ShapeDtypeStruct((12, 64, 128), F32),
-            jax.ShapeDtypeStruct((3072, 128), F32),
+            jax.ShapeDtypeStruct((PACK, 128), BF),
         ],
         in_specs=[vmem] * 12,
         out_specs=[vmem] * 2,
@@ -937,25 +974,27 @@
 
 
 def unpack_kernel(
-    scale, fine_in, whole, fine, out_w1, out_w2, out_w3, out_w4, out_w5, out_b1, out_b2, out_b3, out_b4, out_b5
+    scale, fine_in, whole_in, fine, out_w1, out_w2, out_w3, out_w4, out_w5, out_b1, out_b2, out_b3, out_b4, out_b5, whole
 ):
     fine[...] = fine_in[...]
-    for index, target in ((0, out_w4), (1280, out_w3)):
-        target[:, 0:128] = whole[index : index + 576, :] * scale
-        target[:, 128:256] = whole[index + 576 : index + 1152, :] * scale
+    whole[...] = whole_in[...].astype(F32) * scale
+    for index, target in ((0, out_w4), (1152, out_w3)):
+        target[:, 0:128] = whole[index : index + 576, :]
+        target[:, 128:256] = whole[index + 576 : index + 1152, :]
     for tap in range(9):
         lanes = slice(64 * (tap % 2), 64 * (tap % 2) + 64)
-        at = 2560 + 64 * (tap // 2)
-        out_w2[tap * 64 : tap * 64 + 64, :] = whole[at : at + 64, lanes] * scale
-        at = 16 * (tap // 2)
-        out_w1[tap] = whole[2880 + at : 2892 + at, lanes] * scale
-        out_w5[tap] = whole[1152 + at : 1164 + at, lanes] * scale
-    for index, target in ((1232, out_b4), (2432, out_b3)):
-        target[:, 0:128] = whole[index : index + 1, :] * scale
-        target[:, 128:256] = whole[index + 1 : index + 2, :] * scale
-    out_b2[...] = whole[2960:2961, 0:64] * scale
-    out_b1[...] = whole[2960:2961, 64:128] * scale
-    out_b5[...] = whole[1234:1235, 0:12] * scale
+        at = 2304 + 64 * (tap // 2)
+        out_w2[tap * 64 : tap * 64 + 64, :] = whole[at : at + 64, lanes]
+        first, side = first_place(tap)
+        out_w1[tap] = whole[first : first + 12, side]
+        first, side = last_place(tap)
+        out_w5[tap] = whole[first : first + 12, side]
+    for index, target in ((2720, out_b4), (2722, out_b3)):
+        target[:, 0:128] = whole[index : index + 1, :]
+        target[:, 128:256] = whole[index + 1 : index + 2, :]
+    out_b2[...] = whole[2724:2725, 0:64]
+    out_b1[...] = whole[2724:2725, 64:128]
+    out_b5[...] = whole[2725:2726, 0:12]
 
 
 def unpack_of(fine, whole, scale):
@@ -967,6 +1006,7 @@
         out_shape=[jax.ShapeDtypeStruct(shape, F32) for shape in shapes],
         in_specs=[vmem] * 2,
         out_specs=[vmem] * 11,
+        scratch_shapes=[pltpu.VMEM((PACK, 128), F32)],
         name="unpack",
     )(fine, whole)
 

time: 81.2 us -> 74.3 us (0.915)
  Pallas kernels: 80.3 us -> 73.5 us
    pallas_call x1, Pallas kernels: 77.4 us -> 70.8 us  [train_of(): pl.pallas_call(train_kernel, out_shape=[jax.ShapeDtypeStruct((12, 64, 128...]
where the time goes in v2:
time: 74.3 us; the launch traced here: 74.1 us
  Pallas kernels  73.5 us (99%)
    pallas_call x1, Pallas kernels, train_of(): pl.pallas_call(train_kernel, out_shape=[jax.ShapeDtypeStruct((12, 64, 128...  70.8 us
    pallas_call x1, Pallas kernels, unpack_of(): pl.pallas_call(functools.partial(unpack_kernel, scale), out_shape=[jax.Sh...  2.67 us

profile of v2, /device:TPU:1, one launch (start us, length us, event | category | flops | bytes accessed | tf_op | source)
XLA Modules:
  0.0 74.1 jit_solution(15255244173791403850)
XLA Ops:
  0.6 70.8 %train_tile.1 = (f32[12,64,128]{2,1,0:T(8,128)}, bf16[2816,128]{1,0:T(8,128)(2,1)}) custom-call(bf16[12,512]{1,0:T(8,128)(2,1)} %bitcast.30, bf16[12,64,128]{2,1,0:T(8,128)(2,1)} %cot.1, bf16[9,12,64]{2,1,0:T(8,128)(2,1)} %bitcast.28, bf16[576,64]{1,0:T(8,128)(2,1)} %bitcast.27, bf16[576,256]{1,0:T(8,128)(2,1)} %bitcast.25, bf16[576,256]{1,0:T(8,128)(2,1)} %bitcast.26, ...), custom_call_target="tpu_custom_call" | custom-call | tf_op jit(solution)/shard_map/train_tile/pallas_call | solution.py:959
  71.4 2.7 %unpack.1 = (f32[12,64,128]{2,1,0:T(8,128)}, f32[9,12,64]{2,1,0:T(8,128)}, f32[576,64]{1,0:T(8,128)}, f32[576,256]{1,0:T(8,128)}, f32[576,256]{1,0:T(8,128)}, /*...) custom-call(f32[12,64,128]{2,1,0:T(8,128)} %get-tuple-element.24.fin, ...), custom_call_target="tpu_custom_call" | custom-call | tf_op jit(solution)/shard_map/unpack/pallas_call | solution.py:1004

commit v3 on v2

--- a/solution.py
+++ b/solution.py
@@ -191,6 +191,11 @@
         block = self.whole.at[rows_at(row, self.eighth)]
         self.to_eight(lambda slot, chunk: (block, block))
 
+    def settle(self):
+        for copy in self.sent[: len(self.sent) - len(self.now)]:
+            copy.wait_send()
+        self.sent = list(self.now)
+
     def drain(self):
         for copy in self.sent:
             copy.wait_send()
@@ -381,113 +386,6 @@
     ]
     for copy in locals_:
         copy.start()
-    pl.semaphore_wait(barrier, 47 + len(helpers))
-
-    def remote(src, dst, send_sem, recv_sem, target):
-        return pltpu.make_async_remote_copy(
-            src_ref=src,
-            dst_ref=dst,
-            send_sem=send_sem,
-            recv_sem=recv_sem,
-            device_id=target,
-            device_id_type=MESH_ID,
-        )
-
-    def row_copy(step, dst_row, send_sem, recv_sem, step_x):
-        target = peer(step_x, step)
-        return remote(
-            coarse.at[:, pl.ds(window(target[1]), 256)],
-            rows_in.at[dst_row],
-            send_sem,
-            recv_sem,
-            target,
-        )
-
-    cot_copies = []
-    parts = ((16, 48, 0), (64, 0, 16), (16, 0, 80))
-    for index_x, step_x in enumerate((1, 0, -1)):
-        count, src_row, dst_row = parts[index_x]
-        for index_y, step_y in enumerate((1, 0, -1)):
-            if step_x == 0 and step_y == 0:
-                continue
-            cot_copies.append(
-                remote(
-                    cot.at[:, pl.ds(src_row, count), :],
-                    cot_in.at[index_y, :, pl.ds(dst_row, count), :],
-                    cot_send.at[index_x, index_y],
-                    cot_recv.at[index_x, index_y],
-                    peer(step_x, step_y),
-                )
-            )
-    for copy in cot_copies:
-        copy.start()
-
-    copies = []
-    for step in range(1, 16):
-        copies.append(row_copy(step, 6 + gy, row_send.at[step], row_recv.at[step], 0))
-    for copy in copies:
-        copy.start()
-
-    def far(step_x, dst_row, slot):
-        return [
-            row_copy(step, dst_row, far_send.at[step], far_recv.at[slot], step_x)
-            for step in range(16)
-        ]
-
-    @pl.when(gy < 6)
-    def _():
-        for copy in far(-1, 22 + gy, 6 + gy):
-            copy.start()
-
-    @pl.when(gy >= 10)
-    def _():
-        for copy in far(1, gy - 10, gy - 10):
-            copy.start()
-
-    def await_rows():
-        locals_[1].wait()
-        for step in range(1, 16):
-            row_copy(
-                step, 6 + (gy - step + 16) % 16, row_send.at[step], row_recv.at[step], 0
-            ).wait_recv()
-        for slot in range(12):
-            dst_row = slot if slot < 6 else 16 + slot
-            row_copy(1, dst_row, far_send.at[0], far_recv.at[slot], 0).wait_recv()
-
-    def await_cot():
-        locals_[0].wait()
-        for copy in cot_copies:
-            copy.wait_recv()
-
-    def drain_gather():
-        for copy in copies + cot_copies:
-            copy.wait_send()
-
-        @pl.when(gy < 6)
-        def _():
-            for copy in far(-1, 22 + gy, 6 + gy):
-                copy.wait_send()
-
-        @pl.when(gy >= 10)
-        def _():
-            for copy in far(1, gy - 10, gy - 10):
-                copy.wait_send()
-
-
-    flows = [
-        Flow(number, spot_now, core, pack, whole, *FLOWS[number])
-        for number in range(len(FLOWS))
-    ]
-    refs = (in_a, sum_a, in_b, in_c, in_d)
-    sems = (hop_send, hop_recv)
-    for flow in flows:
-        flow.refs = refs
-        flow.sems = sems
-
-    def progress(numbers, stage):
-        for number in numbers:
-            flows[number].advance(stage)
-
     base_row = gx * 16
     base_col = gy * 32
 
@@ -545,27 +443,119 @@
             v3b[u, :, v * 256 : v * 256 + 256] = v3[tap : tap + 64, :]
             v2b[u, :, v * 64 : v * 64 + 64] = w2[tap : tap + 64, :]
 
+    pl.semaphore_wait(barrier, 47 + len(helpers))
+
+    def remote(src, dst, send_sem, recv_sem, target):
+        return pltpu.make_async_remote_copy(
+            src_ref=src,
+            dst_ref=dst,
+            send_sem=send_sem,
+            recv_sem=recv_sem,
+            device_id=target,
+            device_id_type=MESH_ID,
+        )
+
+    def row_copy(step, dst_row, send_sem, recv_sem, step_x):
+        target = peer(step_x, step)
+        return remote(
+            coarse.at[:, pl.ds(window(target[1]), 256)],
+            rows_in.at[dst_row],
+            send_sem,
+            recv_sem,
+            target,
+        )
+
+    cot_copies = []
+    parts = ((16, 48, 0), (64, 0, 16), (16, 0, 80))
+    for index_x, step_x in enumerate((1, 0, -1)):
+        count, src_row, dst_row = parts[index_x]
+        for index_y, step_y in enumerate((1, 0, -1)):
+            if step_x == 0 and step_y == 0:
+                continue
+            cot_copies.append(
+                remote(
+                    cot.at[:, pl.ds(src_row, count), :],
+                    cot_in.at[index_y, :, pl.ds(dst_row, count), :],
+                    cot_send.at[index_x, index_y],
+                    cot_recv.at[index_x, index_y],
+                    peer(step_x, step_y),
+                )
+            )
+    for copy in cot_copies:
+        copy.start()
+
+    copies = []
+    for step in range(1, 16):
+        copies.append(row_copy(step, 6 + gy, row_send.at[step], row_recv.at[step], 0))
+    for copy in copies:
+        copy.start()
+
+    def far(step_x, dst_row, slot):
+        return [
+            row_copy(step, dst_row, far_send.at[step], far_recv.at[slot], step_x)
+            for step in range(16)
+        ]
+
+    @pl.when(gy < 6)
+    def _():
+        for copy in far(-1, 22 + gy, 6 + gy):
+            copy.start()
+
+    @pl.when(gy >= 10)
+    def _():
+        for copy in far(1, gy - 10, gy - 10):
+            copy.start()
+
+    def await_rows():
+        locals_[1].wait()
+        for step in range(1, 16):
+            row_copy(
+                step, 6 + (gy - step + 16) % 16, row_send.at[step], row_recv.at[step], 0
+            ).wait_recv()
+        for slot in range(12):
+            dst_row = slot if slot < 6 else 16 + slot
+            row_copy(1, dst_row, far_send.at[0], far_recv.at[slot], 0).wait_recv()
+
+    def await_cot():
+        locals_[0].wait()
+        for copy in cot_copies:
+            copy.wait_recv()
+
+    def drain_gather():
+        for copy in copies + cot_copies:
+            copy.wait_send()
+
+        @pl.when(gy < 6)
+        def _():
+            for copy in far(-1, 22 + gy, 6 + gy):
+                copy.wait_send()
+
+        @pl.when(gy >= 10)
+        def _():
+            for copy in far(1, gy - 10, gy - 10):
+                copy.wait_send()
+
+
+    flows = [
+        Flow(number, spot_now, core, pack, whole, *FLOWS[number])
+        for number in range(len(FLOWS))
+    ]
+    refs = (in_a, sum_a, in_b, in_c, in_d)
+    sems = (hop_send, hop_recv)
+    for flow in flows:
+        flow.refs = refs
+        flow.sems = sems
+
+    def progress(numbers, stage):
+        for number in numbers:
+            flows[number].advance(stage)
+
     def spread_out(width, group):
         lanes = iota((12, width), 1)
         spread = one_hot((lanes - over(lanes, group) * group) == iota((12, width), 0))
         for tap in range(9):
             wide[tap * 64 : tap * 64 + 64, 0:width] = mm_tn(w5[tap], spread)
 
-    spread_out(256, 16)
-    lanes5 = iota((64, 256), 1)
-    cell5 = over(lanes5, 16)
-    col5 = over(cell5, 4)
-    row5 = cell5 - col5 * 4
-    for t in range(6):
-        for position, v in enumerate(FINE_ORDER):
-            value = jnp.zeros((64, 256), F32)
-            for r in range(max(0, t - 3), min(2, t) + 1):
-                for s in range(max(0, v - 3), min(2, v) + 1):
-                    tap = (r * 3 + s) * 64
-                    value = jnp.where(
-                        (row5 == t - r) & (col5 == v - s), wide[tap : tap + 64, 0:256], value
-                    )
-            v5f[t, position * 64 : position * 64 + 64, :] = value.astype(BF)
     spread_out(432, 12)
     lanes6 = iota((64, 432), 1)
     cell6 = over(lanes6, 12)
@@ -874,6 +864,21 @@
             pack[at : at + 12, lanes] = term[s * 48 + r * 16 : s * 48 + r * 16 + 12, :]
     progress(OTHERS, 0)
 
+    spread_out(256, 16)
+    lanes5 = iota((64, 256), 1)
+    cell5 = over(lanes5, 16)
+    col5 = over(cell5, 4)
+    row5 = cell5 - col5 * 4
+    for t in range(6):
+        for position, v in enumerate(FINE_ORDER):
+            value = jnp.zeros((64, 256), F32)
+            for r in range(max(0, t - 3), min(2, t) + 1):
+                for s in range(max(0, v - 3), min(2, v) + 1):
+                    tap = (r * 3 + s) * 64
+                    value = jnp.where(
+                        (row5 == t - r) & (col5 == v - s), wide[tap : tap + 64, 0:256], value
+                    )
+            v5f[t, position * 64 : position * 64 + 64, :] = value.astype(BF)
     z = jnp.zeros((512, 256), F32)
     for t in range(6):
         big_r, d = FINE_SOURCE[t]
@@ -896,14 +901,20 @@
     progress(LAYER_THREE, 3)
     for o in range(12):
         fine[o] = lined[pl.ds(o, 64, stride=16), :] + b5[0:1, o : o + 1]
+    drain_gather()
     progress(OTHERS, 2)
+    for number in LAYER_FOUR:
+        flows[number].settle()
     progress(LAYER_FOUR, 5)
     progress(LAYER_THREE, 4)
+    for number in LAYER_THREE + OTHERS:
+        flows[number].settle()
+    for number in LAYER_FOUR:
+        flows[number].drain()
     progress(OTHERS, 3)
     progress(LAYER_THREE, 5)
-    drain_gather()
-    for flow in flows:
-        flow.drain()
+    for number in LAYER_THREE + OTHERS:
+        flows[number].drain()
 
 
 def train_of(coarse, cot, weights, biases):

time: 74.3 us -> 73.9 us (level)
  no operation moved by 1% of the time
where the time goes in v3:
time: 73.9 us; the launch traced here: 73.7 us
  Pallas kernels  73 us (99%)
    pallas_call x1, Pallas kernels, train_of(): pl.pallas_call(train_kernel, out_shape=[jax.ShapeDtypeStruct((12, 64, 128...  70.4 us
    pallas_call x1, Pallas kernels, unpack_of(): pl.pallas_call(functools.partial(unpack_kernel, scale), out_shape=[jax.Sh...  2.67 us

profile of v3, /device:TPU:1, one launch (start us, length us, event | category | flops | bytes accessed | tf_op | source)
XLA Modules:
  0.0 73.7 jit_solution(10048496557055958578)
XLA Ops:
  0.6 70.4 %train_tile.1 = (f32[12,64,128]{2,1,0:T(8,128)}, bf16[2816,128]{1,0:T(8,128)(2,1)}) custom-call(bf16[12,512]{1,0:T(8,128)(2,1)} %bitcast.30, bf16[12,64,128]{2,1,0:T(8,128)(2,1)} %cot.1, bf16[9,12,64]{2,1,0:T(8,128)(2,1)} %bitcast.28, bf16[576,64]{1,0:T(8,128)(2,1)} %bitcast.27, bf16[576,256]{1,0:T(8,128)(2,1)} %bitcast.25, bf16[576,256]{1,0:T(8,128)(2,1)} %bitcast.26, ...), custom_call_target="tpu_custom_call" | custom-call | tf_op jit(solution)/shard_map/train_tile/pallas_call | solution.py:970
  71.0 2.7 %unpack.1 = (f32[12,64,128]{2,1,0:T(8,128)}, f32[9,12,64]{2,1,0:T(8,128)}, f32[576,64]{1,0:T(8,128)}, f32[576,256]{1,0:T(8,128)}, f32[576,256]{1,0:T(8,128)}, /*...) custom-call(f32[12,64,128]{2,1,0:T(8,128)} %get-tuple-element.24.fin, ...), custom_call_target="tpu_custom_call" | custom-call | tf_op jit(solution)/shard_map/unpack/pallas_call | solution.py:1015

commit v4 on v3

--- a/solution.py
+++ b/solution.py
@@ -879,19 +879,19 @@
                         (row5 == t - r) & (col5 == v - s), wide[tap : tap + 64, 0:256], value
                     )
             v5f[t, position * 64 : position * 64 + 64, :] = value.astype(BF)
+    progress(LAYER_FOUR, 3)
+    progress(LAYER_THREE, 2)
     z = jnp.zeros((512, 256), F32)
     for t in range(6):
         big_r, d = FINE_SOURCE[t]
         z = z + mm(inner(x5.at[big_r], d, slice(0, 384)), v5f[t])
     z5[...] = z
-    progress(LAYER_FOUR, 3)
-    progress(LAYER_THREE, 2)
+    progress(OTHERS, 1)
     for i in range(16):
         for big_c in range(4):
             turned[big_c * 32 : big_c * 32 + 32, i * 64 : i * 64 + 64] = z5[
                 i * 32 : i * 32 + 32, big_c * 64 : big_c * 64 + 64
             ]
-    progress(OTHERS, 1)
     spot = iota((128, 128), 0)
     column = over(spot, 32)
     weave = one_hot(iota((128, 128), 1) == (spot - column * 32) * 4 + column)

time: 73.9 us -> 74.4 us (level)
  no operation moved by 1% of the time
where the time goes in v4:
time: 74.4 us; the launch traced here: 74.3 us
  Pallas kernels  73.6 us (99%)
    pallas_call x1, Pallas kernels, train_of(): pl.pallas_call(train_kernel, out_shape=[jax.ShapeDtypeStruct((12, 64, 128...  70.9 us
    pallas_call x1, Pallas kernels, unpack_of(): pl.pallas_call(functools.partial(unpack_kernel, scale), out_shape=[jax.Sh...  2.67 us

profile of v4, /device:TPU:1, one launch (start us, length us, event | category | flops | bytes accessed | tf_op | source)
XLA Modules:
  0.0 74.3 jit_solution(12665691321238396127)
XLA Ops:
  0.6 70.9 %train_tile.1 = (f32[12,64,128]{2,1,0:T(8,128)}, bf16[2816,128]{1,0:T(8,128)(2,1)}) custom-call(bf16[12,512]{1,0:T(8,128)(2,1)} %bitcast.30, bf16[12,64,128]{2,1,0:T(8,128)(2,1)} %cot.1, bf16[9,12,64]{2,1,0:T(8,128)(2,1)} %bitcast.28, bf16[576,64]{1,0:T(8,128)(2,1)} %bitcast.27, bf16[576,256]{1,0:T(8,128)(2,1)} %bitcast.25, bf16[576,256]{1,0:T(8,128)(2,1)} %bitcast.26, ...), custom_call_target="tpu_custom_call" | custom-call | tf_op jit(solution)/shard_map/train_tile/pallas_call | solution.py:970
  71.6 2.7 %unpack.1 = (f32[12,64,128]{2,1,0:T(8,128)}, f32[9,12,64]{2,1,0:T(8,128)}, f32[576,64]{1,0:T(8,128)}, f32[576,256]{1,0:T(8,128)}, f32[576,256]{1,0:T(8,128)}, /*...) custom-call(f32[12,64,128]{2,1,0:T(8,128)} %get-tuple-element.24.fin, ...), custom_call_target="tpu_custom_call" | custom-call | tf_op jit(solution)/shard_map/unpack/pallas_call | solution.py:1015
